TPU v7x, 32 devices: a whole 2x2x4 slice. The times are simulated.
32 devices in a mesh: seq: 8 (over y, x, core), tp: 4 (over z).
Axes of the slice: x: 2, y: 2, z: 4, core: 2. Of those that a mesh axis runs over, the one named last changes fastest.
Arguments:
- hidden: bfloat16 [5120, 2048], P('seq', 'tp'), may hold values from -12 to 12
- w_qkv: bfloat16 [3, 2048, 2048], P(None, None, 'tp')
- w_out: bfloat16 [2048, 2048], P('tp'), may hold values from -0.125 to 0.125
- seg_ids: int32 [5120], P('seq'), may hold values from 0 to 16, as said below
- positions: int32 [5120], P('seq'), may hold values from 0 to 4095, as said below
- page_table: int32 [320], P('seq'), may hold values from 0 to 319, as said below
Outputs:
- delta: bfloat16 [5120, 2048], P('seq', 'tp')
- k_cache: bfloat16 [320, 16, 2048], P('seq', None, 'tp')
- v_cache: bfloat16 [320, 16, 2048], P('seq', None, 'tp')
Inputs may be any that keep to these rules, and one draw needn't show every extreme that they name: `seg_ids`: tokens 0 to 4095 form prompt 0; the remaining tokens form prompts 1 to 16 in order, each of 16 to 112 tokens. `positions`: positions rise by one from token to token inside a prompt; prompt 0 starts at 0, every other prompt at a value below 256. `page_table`: every page appears once; page p lives on index p // 40 of seq; the pages of one index of seq go to at most 5 pages of any one owner, and exactly 5 to some owner.
All inputs are finite; a program needn't handle non-finite values.
Results may differ from a plain program's by a relative error of at most 0.0076.
Values may be sent and summed in bfloat16 or wider, within the bound.
A program may use at most 320 MiB of HBM per device.

v0:
```python
import jax
import jax.numpy as jnp
from jax import lax
from jax.sharding import PartitionSpec as P

HEAD_DIM = 128
PAGE = 16


ROPE_BASE = 10000.0
EPSILON = 1e-05
NEG_LARGE = -1e30


def rope_tables(position_ids, head_width):
    half_width = head_width // 2
    frequency = ROPE_BASE ** (-jnp.arange(half_width).astype(jnp.float32) * 2.0 / head_width)
    angle = position_ids.astype(jnp.float32)[:, None] * frequency[None, :]
    return (jnp.cos(angle), jnp.sin(angle))


def rotate(vectors, cosine, sine_part):
    half_width = vectors.shape[-1] // 2
    first_half = vectors[..., :half_width]
    second_half = vectors[..., half_width:]
    cos_rows = cosine[:, None, :]
    sin_rows = sine_part[:, None, :]
    return jnp.concatenate(
        [
            first_half * cos_rows - second_half * sin_rows,
            second_half * cos_rows + first_half * sin_rows,
        ],
        axis=-1,
    )


def fresh_state(query_heads):
    head_count, query_count, head_width = query_heads.shape
    return (
        jnp.full((head_count, query_count), NEG_LARGE, jnp.float32),
        jnp.zeros((head_count, query_count), jnp.float32),
        jnp.zeros((head_count, query_count, head_width), jnp.float32),
    )


def attend_group(state, query_group, kv_piece, key_seg, key_pos):
    query_heads, query_seg, query_pos = query_group
    head_count, query_count, head_width = query_heads.shape
    visible = (key_seg[None, :] == query_seg[:, None]) & (key_pos[None, :] <= query_pos[:, None])

    def attend_piece(current):
        running_max, running_sum, weighted_sum = current
        row_count = kv_piece.shape[0]
        key_heads = kv_piece[:, : head_count * head_width].reshape(
            row_count, head_count, head_width
        )
        value_heads = kv_piece[:, head_count * head_width :].reshape(
            row_count, head_count, head_width
        )
        scores = jnp.einsum(
            "hqe,khe->hqk", query_heads, key_heads, preferred_element_type=jnp.float32
        ) * head_width ** (-0.5)
        scores = jnp.where(visible[None], scores, NEG_LARGE)
        new_max = jnp.maximum(running_max, jnp.max(scores, axis=2))
        weights = jnp.where(visible[None], jnp.exp(scores - new_max[:, :, None]), 0.0)
        new_sum = jnp.sum(weights, axis=2)
        mixed = jnp.einsum(
            "hqk,khe->hqe",
            weights.astype(jnp.bfloat16),
            value_heads,
            preferred_element_type=jnp.float32,
        )
        return (new_max, new_sum, mixed)

    return lax.cond(jnp.any(visible), attend_piece, lambda current: current, state)


def finish(state):
    running_max, running_sum, weighted_sum = state
    return (weighted_sum / running_sum[:, :, None]).astype(jnp.bfloat16)


def write_pages(kv_rows, page_table, width_dev):
    tok_count = kv_rows.shape[0]
    block_count = tok_count // PAGE
    devices = lax.axis_size("seq")
    capacity = (block_count + devices - 1) // devices
    owner = page_table // block_count
    owner_hot = (owner[:, None] == jnp.arange(devices, dtype=jnp.int32)[None, :]).astype(jnp.int32)
    earlier = jnp.cumsum(owner_hot, axis=0) - owner_hot
    occurrence = jnp.sum(earlier * owner_hot, axis=1)
    slot = owner * capacity + occurrence
    slot_hot = slot[None, :] == jnp.arange(devices * capacity, dtype=jnp.int32)[:, None]
    flat_blocks = kv_rows.reshape(block_count, PAGE * 2 * width_dev)
    outgoing = jnp.einsum(
        "sb,bx->sx", slot_hot.astype(jnp.bfloat16), flat_blocks, preferred_element_type=jnp.float32
    ).astype(jnp.bfloat16)
    labels = jnp.sum(jnp.where(slot_hot, (page_table % block_count)[None, :] + 1, 0), axis=1) - 1
    arrived, arrived_labels = (
        lax.all_to_all(outgoing, "seq", split_axis=0, concat_axis=0, tiled=True),
        lax.all_to_all(labels, "seq", split_axis=0, concat_axis=0, tiled=True),
    )
    place_hot = (
        arrived_labels[None, :] == jnp.arange(block_count, dtype=jnp.int32)[:, None]
    ).astype(jnp.bfloat16)
    placed = jnp.einsum("bs,sx->bx", place_hot, arrived, preferred_element_type=jnp.float32).astype(
        jnp.bfloat16
    )
    placed = placed.reshape(block_count, PAGE, 2 * width_dev)
    return (placed[:, :, :width_dev], placed[:, :, width_dev:])


def body(hidden, w_qkv, w_out, seg_ids, positions, page_table):
    tok_count = hidden.shape[0]
    full_rows = lax.all_gather(hidden, "tp", axis=1, tiled=True).astype(jnp.float32)
    row_mean = jnp.mean(full_rows, axis=1, keepdims=True)
    centred = full_rows - row_mean
    row_var = jnp.mean(centred * centred, axis=1, keepdims=True)
    normed = (centred * lax.rsqrt(row_var + EPSILON)).astype(jnp.bfloat16)
    projected = jnp.einsum("td,jde->jte", normed, w_qkv, preferred_element_type=jnp.float32)
    width_dev = w_qkv.shape[2]
    heads_dev = width_dev // HEAD_DIM
    cosine, sine_part = rope_tables(positions, HEAD_DIM)
    queries = rotate(
        projected[0].reshape(tok_count, heads_dev, HEAD_DIM), cosine, sine_part
    ).astype(jnp.bfloat16)
    key_heads = rotate(
        projected[1].reshape(tok_count, heads_dev, HEAD_DIM), cosine, sine_part
    ).astype(jnp.bfloat16)
    values = projected[2].astype(jnp.bfloat16)
    kv_rows = jnp.concatenate([key_heads.reshape(tok_count, width_dev), values], axis=1)
    query_heads = jnp.transpose(queries, (1, 0, 2))
    groups = ((query_heads, seg_ids, positions),)
    states = tuple((fresh_state(query_group[0]) for query_group in groups))

    def fold_plain(fold_state, shard_piece):
        return tuple(
            (
                attend_group(one_state, query_group, shard_piece[0], shard_piece[1], shard_piece[2])
                for one_state, query_group in zip(fold_state, groups)
            )
        )

    states = fold_plain(
        states,
        (
            lax.all_gather(kv_rows, "seq", axis=0, tiled=True),
            lax.all_gather(seg_ids, "seq", axis=0, tiled=True),
            lax.all_gather(positions, "seq", axis=0, tiled=True),
        ),
    )
    k_cache, v_cache = write_pages(kv_rows, page_table, width_dev)
    finished = [finish(one_state) for one_state in states]
    attended_heads = finished[0]
    attended = jnp.transpose(attended_heads, (1, 0, 2)).reshape(tok_count, width_dev)
    partial_out = jnp.dot(attended, w_out, preferred_element_type=jnp.float32)
    delta = lax.psum_scatter(partial_out, "tp", scatter_dimension=1, tiled=True).astype(
        jnp.bfloat16
    )
    return (delta, k_cache, v_cache)


def solution(mesh):
    in_specs = (P("seq", "tp"), P(None, None, "tp"), P("tp", None), P("seq"), P("seq"), P("seq"))
    out_specs = (P("seq", "tp"), P("seq", None, "tp"), P("seq", None, "tp"))
    return jax.shard_map(body, mesh=mesh, in_specs=in_specs, out_specs=out_specs, check_vma=False)
```

profile of v0, /device:TPU:5, one launch (start us, length us, event | category | flops | bytes accessed | tf_op | source)
XLA Modules:
  0.0 344.8 jit_solution(11553467967130344222)
XLA Ops:
  7.2 0.7 all-gather.5.cloned.1.call-update
  8.0 0.7 convert_element_type.52
  8.7 2.1 multiply_cosine_fusion
  10.7 54.6 %all-gather.5.cloned.1.call-done = bf16[640,2048]{1,0:T(8,128)(2,1)} async-done(((bf16[640,512]{1,0:T(8,128)(2,1)}), bf16[640,2048]{1,0:T(8,128)(2,1)}) %all-gather.5.cloned.1.call-update) | async-done | bytes 2621456 | tf_op jit(solution)/shard_map/all_gather | solution.py:115
  65.4 2.3 convert_reduce_fusion
  67.7 0.2 copy-done.3
  67.9 0.8 fusion.11
  68.7 8.0 %fusion.18 = f32[3,640,512]{1,2,0:T(8,128)S(1)} fusion(bf16[3,2048,512]{2,1,0:T(8,128)(2,1)} %param.9, bf16[640,2048]{1,0:T(8,128)(2,1)S(1)} %copy-done.3, f32[640]{0:T(1024)S(1)} %add_rsqrt_fusion, f32[640]{0:T(1024)S(1)} %broadcast_multiply_fusion), kind=kOutput, calls=%fused_computation.24 | convolution fusion | flops 4031774720 | bytes 12850176 | tf_op jit(solution)/shard_map/td,jde->jte/dot_general | solution.py:120
  76.8 0.9 fusion.21
  77.9 1.2 fusion.31
  79.1 1.2 fusion.30
  80.2 1.5 copy.56
  81.7 2.6 copy.54
  84.3 2.6 copy.55
  86.8 2.6 copy.53
  89.4 4.1 %subtract_convert_fusion = (bf16[640,4,64]{2,0,1:T(8,128)(2,1)}, bf16[640,4,64]{2,0,1:T(8,128)(2,1)}, bf16[640,4,64]{2,0,1:T(8,128)(2,1)S(1)}, bf16[640,4,64]{2,0,1:T(8,128)(2,1)S(1)}) fusion(f32[640,4,64]{2,0,1:T(8,128)S(1)} %copy.56, f32[640,4,64]{2,0,1:T(8,128)} %copy.55, f32[640,64]{1,0:T(8,128)} %get-tuple-element.41, f32[640,64]{1,0:T(8,128)} %get-tuple-element.40, ...), kind=kLoop, calls=%fused_computation.29 | loop fusion | flops 2621440 | bytes 4259840 | tf_op jit(solution)/shard_map/convert
  93.5 1.2 pad_maximum_fusion.1
  94.7 1.4 copy.42
  96.1 1.2 pad_maximum_fusion
  97.4 9.8 %all-gather.1 = s32[8,1,640]{2,1,0:T(1,128)S(1)} all-gather(s32[1,1,640]{2,1,0:T(1,128)S(1)} %reshape.125), channel_id=1, replica_groups=mesh['seq'=8,'tp'=4] {'seq'}, dimensions={0}, use_global_device_ids=true | all-gather | bytes 23040 | tf_op jit(solution)/shard_map/all_gather | solution.py:149
  107.2 8.5 %all-gather = s32[8,1,640]{2,1,0:T(1,128)S(1)} all-gather(s32[1,1,640]{2,1,0:T(1,128)S(1)} %reshape.123), channel_id=1, replica_groups=mesh['seq'=8,'tp'=4] {'seq'}, dimensions={0}, use_global_device_ids=true | all-gather | bytes 23040 | tf_op jit(solution)/shard_map/all_gather | solution.py:148
  115.7 5.7 %fusion.26 = (pred[]{:T(512)}, pred[640,5120]{1,0:T(8,128)(4,1)}) fusion(s32[640]{0:T(1024)S(1)} %copy-done.8, s32[5120]{0:T(1024)S(1)} %bitcast.41, s32[640]{0:T(1024)S(1)} %copy-done.9, s32[5120]{0:T(1024)S(1)} %bitcast.42), kind=kLoop, calls=%fused_computation.53 | loop fusion | flops 13107199 | bytes 3322881 | tf_op jit(solution)/shard_map/reduce_or | solution.py:75
  122.0 1.2 maximum_bitcast_fusion
  123.2 36.2 %all-gather.7.cloned.1.call-done = bf16[5120,1024]{0,1:T(8,128)(2,1)} async-done(((bf16[640,1024]{0,1:T(8,128)(2,1)}), bf16[5120,1024]{0,1:T(8,128)(2,1)}) %all-gather.7.cloned.1.call-update) | async-done | bytes 10485776 | tf_op jit(solution)/shard_map/all_gather | solution.py:147
  159.5 78.7 %conditional.1 = (f32[4,640]{1,0:T(4,128)S(1)}, f32[4,640,128]{1,2,0:T(8,128)S(1)}) conditional(s32[]{:T(128)} %convert_element_type.49, () %tuple.16, (pred[640,5120]{1,0:T(8,128)(4,1)}, bf16[5120,1024]{0,1:T(8,128)(2,1)}, bf16[4,640,128]{2,1,0:T(8,128)(2,1)}) %tuple.17), branch_computations={%region_3.0_spmd, %region_4.7_spmd} | conditional | flops 6881277440 | bytes 216330320 | solution.py:75
  159.5 8.8 %fusion.27 = (bf16[5120,512]{0,1:T(8,128)(2,1)}, bf16[5120,512]{0,1:T(8,128)(2,1)}) fusion(bf16[5120,1024]{0,1:T(8,128)(2,1)} %get-tuple-element.8), kind=kLoop, calls=%fused_computation.54 | loop fusion | bytes 20971520 | tf_op jit(solution)/shard_map/cond/branch_1_fun/slice | solution.py:57
  168.3 22.6 %fusion = (f32[4,640]{1,0:T(4,128)S(1)}, f32[4,640,5120]{2,1,0:T(8,128)}) fusion(pred[640,5120]{1,0:T(8,128)(4,1)} %get-tuple-element.6, bf16[4,640,128]{2,1,0:T(8,128)(2,1)S(1)} %copy-done.7, bf16[5120,4,128]{0,2,1:T(8,128)(2,1)} %bitcast.34), kind=kOutput, calls=%fused_computation.2 | convolution fusion | flops 3394762240 | bytes 61614080 | tf_op jit(solution)/shard_map/cond/branch_1_fun/hqe,khe->hqk/dot_general | solution.py:60
  190.9 22.4 %fusion.3 = f32[4,640,128]{1,2,0:T(8,128)S(1)} fusion(bf16[5120,4,128]{0,2,1:T(8,128)(2,1)} %bitcast.33, f32[4,640,5120]{2,1,0:T(8,128)} %get-tuple-element.25, f32[4,640]{1,0:T(4,128)S(1)} %broadcast_maximum_fusion, pred[640,5120]{1,0:T(8,128)(4,1)S(1)} %copy-done.1), kind=kOutput, calls=%fused_computation.5 | convolution fusion | flops 3420979200 | bytes 62269440 | tf_op jit(solution)/shard_map/cond | solution.py:75
  213.3 24.9 %fusion.2 = f32[4,640]{1,0:T(4,128)S(1)} fusion(f32[4,640,5120]{2,1,0:T(8,128)} %get-tuple-element.25, f32[4,640]{1,0:T(4,128)S(1)} %broadcast_maximum_fusion, pred[640,5120]{1,0:T(8,128)(4,1)} %get-tuple-element.6), kind=kLoop, calls=%fused_computation.4 | loop fusion | flops 65533440 | bytes 55726080 | tf_op jit(solution)/shard_map/cond/branch_1_fun/reduce_sum | solution.py:66
  238.3 3.9 %fusion.32 = f32[640,2048]{1,0:T(8,128)} fusion(bf16[640,512]{0,1:T(8,128)(2,1)S(1)} %bitcast.39, bf16[512,2048]{1,0:T(8,128)(2,1)S(1)} %copy-done), kind=kOutput, calls=%fused_computation.59 | convolution fusion | flops 1342177280 | bytes 7995392 | tf_op jit(solution)/shard_map/dot_general | solution.py:156
  242.2 0.6 copy-done.10
  243.0 0.2 select_reduce_fusion.1
  243.3 0.7 sub.44
  244.0 4.0 %all-to-all-start = ((s32[8,5,1]{1,2,0:T(1,128)}), s32[8,5,1]{1,2,0:T(1,128)S(1)}, u32[]{:S(2)}, u32[]{:S(2)}) async-start(s32[8,5,1]{1,2,0:T(1,128)} %bitcast.13), calls=%async_computation.1 | async-start | bytes 8192 | tf_op jit(solution)/shard_map/all_to_all | solution.py:101
  248.0 1.6 copy.47
  249.6 2.5 reshape.121
  252.1 1.6 convolution_convert_fusion.1
  253.7 3.3 all_to_all.13
  257.0 4.3 %all-to-all-start.1 = ((bf16[8,5,16384]{2,1,0:T(8,128)(2,1)}), bf16[8,5,16384]{2,1,0:T(8,128)(2,1)}, u32[]{:S(2)}, u32[]{:S(2)}) async-start(bf16[8,5,16384]{2,1,0:T(8,128)(2,1)} %all_to_all.13), calls=%async_computation.2 | async-start | bytes 4194304 | tf_op jit(solution)/shard_map/all_to_all | solution.py:100
  261.3 0.5 broadcast.109
  261.8 0.7 reduce.3
  262.6 21.6 %all-to-all-done.1 = bf16[8,5,16384]{2,1,0:T(8,128)(2,1)} async-done(((bf16[8,5,16384]{2,1,0:T(8,128)(2,1)}), bf16[8,5,16384]{2,1,0:T(8,128)(2,1)}, u32[]{:S(2)}, u32[]{:S(2)}) %all-to-all-start.1) | async-done | bytes 1310752 | tf_op jit(solution)/shard_map/all_to_all | solution.py:100
  284.1 2.2 all_to_all.15
  286.4 0.5 convolution_convert_fusion
  286.9 0.7 copy.57
  287.6 1.2 fusion.29
  288.8 47.2 %reduce-scatter.2.cloned.1.call-done = f32[640,512]{1,0:T(8,128)} async-done(((f32[640,2048]{1,0:T(8,128)}), f32[640,512]{1,0:T(8,128)}) %reduce-scatter.2.cloned.1.call-update) | async-done | bytes 1310736 | tf_op jit(solution)/shard_map/reduce_scatter | solution.py:157
  336.0 2.2 convert_element_type.57
  (41 shorter events, 0.9 us)
Async XLA Ops:
  7.2 231.1 %copy-start = (bf16[512,2048]{1,0:T(8,128)(2,1)S(1)}, bf16[512,2048]{1,0:T(8,128)(2,1)}, u32[]{:S(2)}) copy-start(bf16[512,2048]{1,0:T(8,128)(2,1)} %param.10) | copy-start | bytes 6291460
  7.2 58.2 %all-gather.5.cloned.1.call-start = ((), (), s32[]{:S(2)}) async-start(), calls=%async_computation.3 | async-start | bytes 3276800 | tf_op jit(solution)/shard_map/all_gather | solution.py:115
  7.9 151.6 %all-gather.7.cloned.1.call-start = ((), (), s32[]{:S(2)}) async-start(), calls=%async_computation.4 | async-start | bytes 11796480 | tf_op jit(solution)/shard_map/all_gather | solution.py:147
  65.4 2.5 copy-start.3
  93.5 2.6 copy-start.6
  94.7 2.7 copy-start.8
  94.7 2.7 copy-start.9
  97.3 24.7 %copy-start.4 = (bf16[640,4,64]{2,0,1:T(8,128)(2,1)S(1)}, bf16[640,4,64]{2,0,1:T(8,128)(2,1)}, u32[]{:S(2)}) copy-start(bf16[640,4,64]{2,0,1:T(8,128)(2,1)} %get-tuple-element.28) | copy-start | bytes 983044
  97.3 24.8 %copy-start.5 = (bf16[640,4,64]{2,0,1:T(8,128)(2,1)S(1)}, bf16[640,4,64]{2,0,1:T(8,128)(2,1)}, u32[]{:S(2)}) copy-start(bf16[640,4,64]{2,0,1:T(8,128)(2,1)} %get-tuple-element.29) | copy-start | bytes 983044
  97.3 238.7 %reduce-scatter.2.cloned.1.call-start = ((), (), s32[]{:S(2)}) async-start(), calls=%async_computation.5 | async-start | bytes 6553600 | tf_op jit(solution)/shard_map/reduce_scatter | solution.py:157
  159.5 8.8 %copy-start.7 = (bf16[4,640,128]{2,1,0:T(8,128)(2,1)S(1)}, bf16[4,640,128]{2,1,0:T(8,128)(2,1)}, u32[]{:S(2)}) copy-start(bf16[4,640,128]{2,1,0:T(8,128)(2,1)} %get-tuple-element.7) | copy-start | bytes 1966084 | tf_op jit(solution)/shard_map/cond
  168.3 22.6 %copy-start.1 = (pred[640,5120]{1,0:T(8,128)(4,1)S(1)}, pred[640,5120]{1,0:T(8,128)(4,1)}, u32[]{:S(2)}) copy-start(pred[640,5120]{1,0:T(8,128)(4,1)} %get-tuple-element.6) | copy-start | bytes 9830404 | tf_op jit(solution)/shard_map/cond
  242.2 0.7 copy-start.10
  242.2 5.8 %copy-start.2 = (bf16[640,1024]{0,1:T(8,128)(2,1)S(1)}, bf16[640,1024]{0,1:T(8,128)(2,1)}, u32[]{:S(2)}) copy-start(bf16[640,1024]{0,1:T(8,128)(2,1)} %pad_maximum_fusion) | copy-start | bytes 3932164
  244.0 13.0 %all-to-all-start = ((s32[8,5,1]{1,2,0:T(1,128)}), s32[8,5,1]{1,2,0:T(1,128)S(1)}, u32[]{:S(2)}, u32[]{:S(2)}) async-start(s32[8,5,1]{1,2,0:T(1,128)} %bitcast.13), calls=%async_computation.1 | async-start | bytes 8192 | tf_op jit(solution)/shard_map/all_to_all | solution.py:101
  257.0 27.2 %all-to-all-start.1 = ((bf16[8,5,16384]{2,1,0:T(8,128)(2,1)}), bf16[8,5,16384]{2,1,0:T(8,128)(2,1)}, u32[]{:S(2)}, u32[]{:S(2)}) async-start(bf16[8,5,16384]{2,1,0:T(8,128)(2,1)} %all_to_all.13), calls=%async_computation.2 | async-start | bytes 4194304 | tf_op jit(solution)/shard_map/all_to_all | solution.py:100
Sparse Core Ops, SparseCore 0:
  9.6 55.7 all-gather.4
  97.4 62.0 all-gather.6
  242.3 93.6 reduce-scatter.1
where the time goes:
time: 347 us; the launch traced here: 345 us
  waiting for transfers between devices  160 us (46%)
  matrix products  59 us (17%)
  other arithmetic  47.6 us (14%)
  local copies, waits for them, and re-layouts  36.5 us (11%)
  blocking collectives  18.3 us (5%)
  between operations  14.6 us (4%)
  starting transfers between devices  8.47 us (2%)
    all_gather x1, waiting for transfers between devices, body(): lax.all_gather(hidden, 'tp', axis=1, tiled=True).astype(jnp.float32)  54.6 us
    reduce_scatter x1, waiting for transfers between devices, body(): lax.psum_scatter(partial_out, 'tp', scatter_dimension=1, tiled=True)  47.2 us
    all_gather x1, waiting for transfers between devices, body(): lax.all_gather(kv_rows, 'seq', axis=0, tiled=True)  36.2 us
    reduce_sum x1, other arithmetic, attend_piece(): new_sum = jnp.sum(weights, axis=2)  24.9 us
    dot_general x1, matrix products, attend_piece(): jnp.einsum('hqe,khe->hqk', query_heads, key_heads, preferred_element_type...  22.6 us
    cond x1, matrix products, attend_group(): lax.cond(jnp.any(visible), attend_piece, lambda current: current, state)  22.4 us
    all_to_all x1, waiting for transfers between devices, write_pages(): lax.all_to_all(outgoing, 'seq', split_axis=0, concat_axis=0, tiled=True)  21.6 us
    unnamed x25, local copies, waits for them, and re-layouts  10.8 us
  transfers between devices with their start and end apart: 5, of which 4 were waited for; matrix products, arithmetic and copies ran while one was open for 6% of the time, Pallas kernels for 0%

commit v1 on v0

--- a/solution.py
+++ b/solution.py
@@ -141,22 +141,28 @@
             )
         )
 
-    states = fold_plain(
-        states,
-        (
-            lax.all_gather(kv_rows, "seq", axis=0, tiled=True),
-            lax.all_gather(seg_ids, "seq", axis=0, tiled=True),
-            lax.all_gather(positions, "seq", axis=0, tiled=True),
-        ),
+    seq_count = lax.axis_size("seq")
+    int_rows = jnp.concatenate([seg_ids, positions, page_table])
+    int_all = lax.all_gather(int_rows, "seq", axis=0, tiled=False)
+    seg_all = int_all[:, :tok_count].reshape(-1)
+    pos_all = int_all[:, tok_count : 2 * tok_count].reshape(-1)
+    table_all = int_all[:, 2 * tok_count :].reshape(-1)
+    kv_all = lax.all_gather(kv_rows, "seq", axis=0, tiled=True)
+    states = fold_plain(states, (kv_all, seg_all, pos_all))
+    block_count = tok_count // PAGE
+    total_blocks = block_count * seq_count
+    inverse = jnp.zeros((total_blocks,), jnp.int32).at[table_all].set(
+        jnp.arange(total_blocks, dtype=jnp.int32)
     )
-    k_cache, v_cache = write_pages(kv_rows, page_table, width_dev)
+    mine = lax.dynamic_slice(inverse, (lax.axis_index("seq") * block_count,), (block_count,))
+    placed = jnp.take(kv_all.reshape(total_blocks, PAGE, 2 * width_dev), mine, axis=0)
+    k_cache = placed[:, :, :width_dev]
+    v_cache = placed[:, :, width_dev:]
     finished = [finish(one_state) for one_state in states]
     attended_heads = finished[0]
     attended = jnp.transpose(attended_heads, (1, 0, 2)).reshape(tok_count, width_dev)
-    partial_out = jnp.dot(attended, w_out, preferred_element_type=jnp.float32)
-    delta = lax.psum_scatter(partial_out, "tp", scatter_dimension=1, tiled=True).astype(
-        jnp.bfloat16
-    )
+    partial_out = jnp.dot(attended, w_out, preferred_element_type=jnp.float32).astype(jnp.bfloat16)
+    delta = lax.psum_scatter(partial_out, "tp", scatter_dimension=1, tiled=True)
     return (delta, k_cache, v_cache)
 
 

time: 347 us -> 303 us (0.87)
  waiting for transfers between devices: 160 us -> 114 us
  local copies, waits for them, and re-layouts: 36.5 us -> 46.7 us
  starting transfers between devices: 8.47 us -> 0.12 us
  blocking collectives: 18.3 us -> 23.2 us
    unnamed x0 -> x1, blocking collectives: none -> 23.2 us
    all_to_all x2 -> x0, waiting for transfers between devices: 21.6 us -> none  [the longest x1 21.6 us: write_pages(): lax.all_to_all(outgoing, 'seq', split_axis=0, concat_axis=0, tiled=True)]
    reduce_scatter x1, waiting for transfers between devices: 47.2 us -> 28.3 us  [body(): delta = lax.psum_scatter(partial_out, 'tp', scatter_dimension=1, tiled=True)]
    all_gather x2 -> x0, blocking collectives: 18.3 us -> none  [the longest x1 9.82 us: body(): lax.all_gather(positions, 'seq', axis=0, tiled=True)]
    all_gather x0 -> x2, local copies, waits for them, and re-layouts: none -> 14.5 us  [the longest x1 14.4 us: body(): kv_all = lax.all_gather(kv_rows, 'seq', axis=0, tiled=True)]
    all_to_all x2 -> x0, starting transfers between devices: 8.35 us -> none  [the longest x1 4.34 us: write_pages(): lax.all_to_all(outgoing, 'seq', split_axis=0, concat_axis=0, tiled=True)]
    all_gather x1, waiting for transfers between devices: 36.2 us -> 30.2 us  [body(): kv_all = lax.all_gather(kv_rows, 'seq', axis=0, tiled=True)]
    all_to_all x3 -> x0, local copies, waits for them, and re-layouts: 6.03 us -> none  [the longest x2 5.52 us: write_pages(): lax.all_to_all(outgoing, 'seq', split_axis=0, concat_axis=0, tiled=True)]
  transfers between devices with their start and end apart: 5 -> 3, of which waited for: 4 -> 3; matrix products, arithmetic and copies ran while one was open for 6% -> 11% of each run, Pallas kernels for 0% -> 0%
where the time goes in v1:
time: 303 us; the launch traced here: 300 us
  waiting for transfers between devices  114 us (38%)
  matrix products  56.1 us (19%)
  local copies, waits for them, and re-layouts  46.7 us (15%)
  other arithmetic  45.2 us (15%)
  blocking collectives  23.2 us (8%)
  between operations  15.3 us (5%)
    all_gather x1, waiting for transfers between devices, body(): lax.all_gather(hidden, 'tp', axis=1, tiled=True).astype(jnp.float32)  54.6 us
    all_gather x1, waiting for transfers between devices, body(): kv_all = lax.all_gather(kv_rows, 'seq', axis=0, tiled=True)  30.2 us
    reduce_scatter x1, waiting for transfers between devices, body(): delta = lax.psum_scatter(partial_out, 'tp', scatter_dimension=1, tiled=True)  28.3 us
    reduce_sum x1, other arithmetic, attend_piece(): new_sum = jnp.sum(weights, axis=2)  24.9 us
    unnamed x1, blocking collectives  23.2 us
    dot_general x1, matrix products, attend_piece(): jnp.einsum('hqe,khe->hqk', query_heads, key_heads, preferred_element_type...  22.6 us
    cond x1, matrix products, attend_group(): lax.cond(jnp.any(visible), attend_piece, lambda current: current, state)  22.3 us
    all_gather x1, local copies, waits for them, and re-layouts, body(): kv_all = lax.all_gather(kv_rows, 'seq', axis=0, tiled=True)  14.4 us
  transfers between devices with their start and end apart: 3, of which 3 were waited for; matrix products, arithmetic and copies ran while one was open for 11% of the time, Pallas kernels for 0%

profile of v1, /device:TPU:5, one launch (start us, length us, event | category | flops | bytes accessed | tf_op | source)
XLA Modules:
  0.0 300.5 jit_solution(12474929699019720682)
XLA Ops:
  7.2 0.0 copy-start
  7.2 0.0 all-gather.4.cloned.1.call-start
  7.2 0.7 all-gather.4.cloned.1.call-update
  7.9 0.0 all-gather.6.cloned.1.call-start
  8.0 0.7 convert_element_type.41
  8.7 2.1 multiply_cosine_fusion
  10.7 54.6 %all-gather.4.cloned.1.call-done = bf16[640,2048]{1,0:T(8,128)(2,1)} async-done(((bf16[640,512]{1,0:T(8,128)(2,1)}), bf16[640,2048]{1,0:T(8,128)(2,1)}) %all-gather.4.cloned.1.call-update) | async-done | bytes 2621456 | tf_op jit(solution)/shard_map/all_gather | solution.py:115
  65.4 2.3 convert_reduce_fusion
  67.7 0.2 copy-done.2
  67.9 0.8 fusion.11
  68.7 8.0 %fusion.18 = f32[3,640,512]{1,2,0:T(8,128)S(1)} fusion(bf16[3,2048,512]{2,1,0:T(8,128)(2,1)} %param.9, bf16[640,2048]{1,0:T(8,128)(2,1)S(1)} %copy-done.2, f32[640]{0:T(1024)S(1)} %add_rsqrt_fusion, f32[640]{0:T(1024)S(1)} %broadcast_multiply_fusion), kind=kOutput, calls=%fused_computation.25 | convolution fusion | flops 4031774720 | bytes 12850176 | tf_op jit(solution)/shard_map/td,jde->jte/dot_general | solution.py:120
  76.8 0.9 fusion.21
  77.7 0.2 fusion.27
  77.9 1.2 fusion.30
  79.0 1.2 fusion.29
  80.2 1.5 copy.34
  81.7 2.6 copy.32
  84.3 2.5 copy.33
  86.8 2.6 copy.31
  89.4 4.1 %subtract_convert_fusion = (bf16[640,4,64]{2,0,1:T(8,128)(2,1)}, bf16[640,4,64]{2,0,1:T(8,128)(2,1)}, bf16[640,4,64]{2,0,1:T(8,128)(2,1)S(1)}, bf16[640,4,64]{2,0,1:T(8,128)(2,1)S(1)}) fusion(f32[640,4,64]{2,0,1:T(8,128)S(1)} %copy.34, f32[640,4,64]{2,0,1:T(8,128)} %copy.33, f32[640,64]{1,0:T(8,128)} %get-tuple-element.45, f32[640,64]{1,0:T(8,128)} %get-tuple-element.44, ...), kind=kLoop, calls=%fused_computation.30 | loop fusion | flops 2621440 | bytes 4259840 | tf_op jit(solution)/shard_map/convert
  93.4 0.4 pad_maximum_fusion.1
  93.8 1.1 copy.21
  94.9 2.6 pad_maximum_fusion
  97.5 0.0 all-gather.6.cloned.1.call-update
  97.5 0.0 reduce-scatter.2.cloned.1.call-start
  97.6 0.6 dynamic-slice
  98.9 0.1 add_dynamic-update-slice_fusion
  99.0 23.2 %all-reduce = s32[10560]{0:T(1024)S(1)} all-reduce(s32[10560]{0:T(1024)S(1)} %add_dynamic-update-slice_fusion), channel_id=2, replica_groups=mesh['seq'=8,'tp'=4] {'seq'}, use_global_device_ids=true, to_apply=%add | all-reduce | flops 10560 | bytes 84480
  122.2 0.1 reshape.150
  122.3 5.7 %fusion.25 = (pred[]{:T(512)}, pred[640,5120]{1,0:T(8,128)(4,1)}) fusion(s32[640]{0:T(1024)S(1)} %copy-done.7, s32[5120]{0:T(1024)S(1)} %le.24, s32[640]{0:T(1024)S(1)} %copy-done.8, s32[5120]{0:T(1024)S(1)} %eq.15), kind=kLoop, calls=%fused_computation.50 | loop fusion | flops 13107199 | bytes 3322881 | tf_op jit(solution)/shard_map/reduce_or | solution.py:75
  128.7 1.2 maximum_bitcast_fusion
  129.9 30.2 %all-gather.6.cloned.1.call-done = bf16[5120,1024]{0,1:T(8,128)(2,1)} async-done(((bf16[640,1024]{0,1:T(8,128)(2,1)}), bf16[5120,1024]{0,1:T(8,128)(2,1)}) %all-gather.6.cloned.1.call-update) | async-done | bytes 10485776 | tf_op jit(solution)/shard_map/all_gather | solution.py:150
  160.1 78.6 %conditional.1 = (f32[4,640]{1,0:T(4,128)S(1)}, f32[4,640,128]{1,2,0:T(8,128)S(1)}) conditional(s32[]{:T(128)} %convert_element_type.38, () %tuple.16, (pred[640,5120]{1,0:T(8,128)(4,1)}, bf16[5120,1024]{0,1:T(8,128)(2,1)}, bf16[4,640,128]{2,1,0:T(8,128)(2,1)}) %tuple.17), branch_computations={%region_3.0_spmd, %region_4.7_spmd} | conditional | flops 6881277440 | bytes 216330320 | solution.py:75
  160.1 8.8 %fusion.26 = (bf16[5120,512]{0,1:T(8,128)(2,1)}, bf16[5120,512]{0,1:T(8,128)(2,1)}) fusion(bf16[5120,1024]{0,1:T(8,128)(2,1)} %get-tuple-element.8), kind=kLoop, calls=%fused_computation.51 | loop fusion | bytes 20971520 | tf_op jit(solution)/shard_map/cond/branch_1_fun/slice | solution.py:57
  168.9 22.6 %fusion = (f32[4,640]{1,0:T(4,128)S(1)}, f32[4,640,5120]{2,1,0:T(8,128)}) fusion(pred[640,5120]{1,0:T(8,128)(4,1)} %get-tuple-element.6, bf16[4,640,128]{2,1,0:T(8,128)(2,1)S(1)} %copy-done.5, bf16[5120,4,128]{0,2,1:T(8,128)(2,1)} %bitcast.30), kind=kOutput, calls=%fused_computation.4 | convolution fusion | flops 3394762240 | bytes 61614080 | tf_op jit(solution)/shard_map/cond/branch_1_fun/hqe,khe->hqk/dot_general | solution.py:60
  191.5 22.3 %fusion.3 = f32[4,640,128]{1,2,0:T(8,128)S(1)} fusion(bf16[5120,4,128]{0,2,1:T(8,128)(2,1)} %bitcast.29, f32[4,640,5120]{2,1,0:T(8,128)} %get-tuple-element.27, f32[4,640]{1,0:T(4,128)S(1)} %broadcast_maximum_fusion, pred[640,5120]{1,0:T(8,128)(4,1)S(1)} %copy-done.1), kind=kOutput, calls=%fused_computation.7 | convolution fusion | flops 3420979200 | bytes 62269440 | tf_op jit(solution)/shard_map/cond | solution.py:75
  213.8 24.9 %fusion.2 = f32[4,640]{1,0:T(4,128)S(1)} fusion(f32[4,640,5120]{2,1,0:T(8,128)} %get-tuple-element.27, f32[4,640]{1,0:T(4,128)S(1)} %broadcast_maximum_fusion, pred[640,5120]{1,0:T(8,128)(4,1)} %get-tuple-element.6), kind=kLoop, calls=%fused_computation.6 | loop fusion | flops 65533440 | bytes 55726080 | tf_op jit(solution)/shard_map/cond/branch_1_fun/reduce_sum | solution.py:66
  238.7 0.1 divide_convert_fusion
  238.8 3.1 %convolution_convert_fusion = bf16[640,2048]{1,0:T(8,128)(2,1)} fusion(bf16[640,512]{0,1:T(8,128)(2,1)S(1)} %bitcast.34, bf16[512,2048]{1,0:T(8,128)(2,1)S(1)} %copy-done), kind=kOutput, calls=%fused_computation.20 | convolution fusion | flops 1343488000 | bytes 5373952 | tf_op jit(solution)/shard_map/dot_general | solution.py:164
  242.0 0.0 reduce-scatter.2.cloned.1.call-update
  242.0 0.1 reshape.132
  242.1 2.9 scatter_custom_fusion
  245.0 0.1 compare_and_fusion.1
  245.1 14.4 %copy.25 = bf16[5120,1024]{1,0:T(8,128)(2,1)} copy(bf16[5120,1024]{0,1:T(8,128)(2,1)} %all-gather.6.cloned.1.call-done) | data formatting | bytes 20971520 | tf_op jit(solution)/shard_map/all_gather | solution.py:150
  259.6 4.7 %gather_fusion = bf16[40,16,1024]{2,1,0:T(8,128)(2,1)S(1)} fusion(bf16[320,16,1024]{2,1,0:T(8,128)(2,1)} %bitcast.28, s32[1024]{0:T(1024)S(1)} %pad_clamp_fusion), kind=kCustom, calls=%fused_computation | custom fusion | bytes 2621600 | tf_op jit(solution)/shard_map/jit(_take)/gather | solution.py:158
  264.2 0.2 broadcast_select_fusion
  264.4 1.2 fusion.28
  265.7 28.3 %reduce-scatter.2.cloned.1.call-done = bf16[640,512]{1,0:T(8,128)(2,1)} async-done(((bf16[640,2048]{1,0:T(8,128)(2,1)}), bf16[640,512]{1,0:T(8,128)(2,1)}) %reduce-scatter.2.cloned.1.call-update) | async-done | bytes 655376 | tf_op jit(solution)/shard_map/reduce_scatter | solution.py:165
  (33 shorter events, 0.1 us)
Async XLA Ops:
  7.2 231.7 %copy-start = (bf16[512,2048]{1,0:T(8,128)(2,1)S(1)}, bf16[512,2048]{1,0:T(8,128)(2,1)}, u32[]{:S(2)}) copy-start(bf16[512,2048]{1,0:T(8,128)(2,1)} %param.10) | copy-start | bytes 6291460
  7.2 58.2 %all-gather.4.cloned.1.call-start = ((), (), s32[]{:S(2)}) async-start(), calls=%async_computation.1 | async-start | bytes 3276800 | tf_op jit(solution)/shard_map/all_gather | solution.py:115
  7.9 152.2 %all-gather.6.cloned.1.call-start = ((), (), s32[]{:S(2)}) async-start(), calls=%async_computation.2 | async-start | bytes 11796480 | tf_op jit(solution)/shard_map/all_gather | solution.py:150
  65.4 2.5 copy-start.2
  93.4 4.1 %copy-start.10 = (u32[32]{0:T(128)S(1)}, u32[32]{0:T(128)}, u32[]{:S(2)}) copy-start(u32[32]{0:T(128)} %constant.59) | copy-start | bytes 388
  93.4 5.4 %copy-start.7 = (s32[640]{0:T(1024)S(1)}, s32[640]{0:T(1024)}, u32[]{:S(2)}) copy-start(s32[640]{0:T(1024)} %param.12) | copy-start | bytes 7684
  93.4 5.4 %copy-start.8 = (s32[640]{0:T(1024)S(1)}, s32[640]{0:T(1024)}, u32[]{:S(2)}) copy-start(s32[640]{0:T(1024)} %param.11) | copy-start | bytes 7684
  93.4 5.4 %copy-start.9 = (s32[40]{0:T(128)S(1)}, s32[40]{0:T(128)}, u32[]{:S(2)}) copy-start(s32[40]{0:T(128)} %param.13) | copy-start | bytes 484
  94.9 33.8 %copy-start.3 = (bf16[640,4,64]{2,0,1:T(8,128)(2,1)S(1)}, bf16[640,4,64]{2,0,1:T(8,128)(2,1)}, u32[]{:S(2)}) copy-start(bf16[640,4,64]{2,0,1:T(8,128)(2,1)} %get-tuple-element.30) | copy-start | bytes 983044
  94.9 33.8 %copy-start.4 = (bf16[640,4,64]{2,0,1:T(8,128)(2,1)S(1)}, bf16[640,4,64]{2,0,1:T(8,128)(2,1)}, u32[]{:S(2)}) copy-start(bf16[640,4,64]{2,0,1:T(8,128)(2,1)} %get-tuple-element.31) | copy-start | bytes 983044
  97.5 196.4 %reduce-scatter.2.cloned.1.call-start = ((), (), s32[]{:S(2)}) async-start(), calls=%async_computation.3 | async-start | bytes 3276800 | tf_op jit(solution)/shard_map/reduce_scatter | solution.py:165
  122.3 37.8 %copy-start.6 = (s32[8,1320]{1,0:T(8,128)}, s32[8,1320]{1,0:T(8,128)S(1)}, u32[]{:S(2)}) copy-start(s32[8,1320]{1,0:T(8,128)S(1)} %reshape.150) | copy-start | bytes 126724
  160.1 8.8 %copy-start.5 = (bf16[4,640,128]{2,1,0:T(8,128)(2,1)S(1)}, bf16[4,640,128]{2,1,0:T(8,128)(2,1)}, u32[]{:S(2)}) copy-start(bf16[4,640,128]{2,1,0:T(8,128)(2,1)} %get-tuple-element.7) | copy-start | bytes 1966084 | tf_op jit(solution)/shard_map/cond
  168.9 22.6 %copy-start.1 = (pred[640,5120]{1,0:T(8,128)(4,1)S(1)}, pred[640,5120]{1,0:T(8,128)(4,1)}, u32[]{:S(2)}) copy-start(pred[640,5120]{1,0:T(8,128)(4,1)} %get-tuple-element.6) | copy-start | bytes 9830404 | tf_op jit(solution)/shard_map/cond
  238.8 3.2 %slice-start = ((s32[8,1320]{1,0:T(8,128)}), s32[8,40]{1,0:T(8,128)S(1)}, s32[]{:S(2)}) async-start(s32[8,1320]{1,0:T(8,128)} %copy-done.6), calls=%async_computation.4 | async-start | bytes 8192 | tf_op jit(solution)/shard_map/slice | solution.py:149
Sparse Core Ops, SparseCore 0:
  9.6 55.7 all-gather.3
  97.6 62.4 all-gather.5
  242.1 51.7 reduce-scatter.1

commit v2 on v1

--- a/solution.py
+++ b/solution.py
@@ -2,6 +2,8 @@
 import jax.numpy as jnp
 from jax import lax
 from jax.sharding import PartitionSpec as P
+from jax.experimental import pallas as pl
+from jax.experimental.pallas import tpu as pltpu
 
 HEAD_DIM = 128
 PAGE = 16
@@ -73,6 +75,87 @@
         return (new_max, new_sum, mixed)
 
     return lax.cond(jnp.any(visible), attend_piece, lambda current: current, state)
+
+
+INTERPRET = False
+
+
+def flash_kernel(need_ref, kid_ref, q_ref, k_ref, v_ref, qseg_ref, qpos_ref, kseg_ref, kpos_ref,
+                 o_ref, m_scr, l_scr, acc_scr):
+    j = pl.program_id(1)
+
+    @pl.when(j == 0)
+    def _():
+        m_scr[...] = jnp.full(m_scr.shape, NEG_LARGE, jnp.float32)
+        l_scr[...] = jnp.zeros(l_scr.shape, jnp.float32)
+        acc_scr[...] = jnp.zeros(acc_scr.shape, jnp.float32)
+
+    @pl.when(need_ref[j] != 0)
+    def _():
+        s = lax.dot_general(
+            q_ref[...], k_ref[...], (((1,), (1,)), ((), ())), preferred_element_type=jnp.float32
+        ) * HEAD_DIM ** (-0.5)
+        vis = (kseg_ref[...] == qseg_ref[...]) & (kpos_ref[...] <= qpos_ref[...])
+        s = jnp.where(vis, s, NEG_LARGE)
+        m_prev = m_scr[...]
+        m_new = jnp.maximum(m_prev, jnp.max(s, axis=1, keepdims=True))
+        alpha = jnp.exp(m_prev - m_new)
+        p = jnp.where(vis, jnp.exp(s - m_new), 0.0)
+        l_scr[...] = alpha * l_scr[...] + jnp.sum(p, axis=1, keepdims=True)
+        acc_scr[...] = alpha * acc_scr[...] + jnp.dot(
+            p.astype(jnp.bfloat16), v_ref[...], preferred_element_type=jnp.float32
+        )
+        m_scr[...] = m_new
+
+    @pl.when(j == pl.num_programs(1) - 1)
+    def _():
+        o_ref[...] = (acc_scr[...] / l_scr[...]).astype(o_ref.dtype)
+
+
+def flash_attend(query_heads, seg_q, pos_q, kv_all, seg_all, pos_all):
+    head_count, query_count, head_width = query_heads.shape
+    key_count = kv_all.shape[0]
+    block_k = query_count
+    block_count = key_count // block_k
+    visible = (seg_all[None, :] == seg_q[:, None]) & (pos_all[None, :] <= pos_q[:, None])
+    need = jnp.any(visible.reshape(query_count, block_count, block_k), axis=(0, 2)).astype(jnp.int32)
+    key_index = lax.cummax(jnp.where(need != 0, jnp.arange(block_count, dtype=jnp.int32), 0), axis=0)
+    grid_spec = pltpu.PrefetchScalarGridSpec(
+        num_scalar_prefetch=2,
+        grid=(head_count, block_count),
+        in_specs=[
+            pl.BlockSpec((None, query_count, head_width), lambda h, j, nd, kd: (h, 0, 0)),
+            pl.BlockSpec((block_k, head_width), lambda h, j, nd, kd: (kd[j], h)),
+            pl.BlockSpec((block_k, head_width), lambda h, j, nd, kd: (kd[j], head_count + h)),
+            pl.BlockSpec((query_count, 1), lambda h, j, nd, kd: (0, 0)),
+            pl.BlockSpec((query_count, 1), lambda h, j, nd, kd: (0, 0)),
+            pl.BlockSpec((1, block_k), lambda h, j, nd, kd: (0, kd[j])),
+            pl.BlockSpec((1, block_k), lambda h, j, nd, kd: (0, kd[j])),
+        ],
+        out_specs=pl.BlockSpec((None, query_count, head_width), lambda h, j, nd, kd: (h, 0, 0)),
+        scratch_shapes=[
+            pltpu.VMEM((query_count, 1), jnp.float32),
+            pltpu.VMEM((query_count, 1), jnp.float32),
+            pltpu.VMEM((query_count, head_width), jnp.float32),
+        ],
+    )
+    return pl.pallas_call(
+        flash_kernel,
+        grid_spec=grid_spec,
+        out_shape=jax.ShapeDtypeStruct(query_heads.shape, jnp.bfloat16),
+        compiler_params=pltpu.CompilerParams(dimension_semantics=("arbitrary", "arbitrary")),
+        interpret=INTERPRET,
+    )(
+        need,
+        key_index,
+        query_heads,
+        kv_all,
+        kv_all,
+        seg_q.reshape(query_count, 1),
+        pos_q.reshape(query_count, 1),
+        seg_all.reshape(1, key_count),
+        pos_all.reshape(1, key_count),
+    )
 
 
 def finish(state):
@@ -130,17 +213,6 @@
     values = projected[2].astype(jnp.bfloat16)
     kv_rows = jnp.concatenate([key_heads.reshape(tok_count, width_dev), values], axis=1)
     query_heads = jnp.transpose(queries, (1, 0, 2))
-    groups = ((query_heads, seg_ids, positions),)
-    states = tuple((fresh_state(query_group[0]) for query_group in groups))
-
-    def fold_plain(fold_state, shard_piece):
-        return tuple(
-            (
-                attend_group(one_state, query_group, shard_piece[0], shard_piece[1], shard_piece[2])
-                for one_state, query_group in zip(fold_state, groups)
-            )
-        )
-
     seq_count = lax.axis_size("seq")
     int_rows = jnp.concatenate([seg_ids, positions, page_table])
     int_all = lax.all_gather(int_rows, "seq", axis=0, tiled=False)
@@ -148,7 +220,7 @@
     pos_all = int_all[:, tok_count : 2 * tok_count].reshape(-1)
     table_all = int_all[:, 2 * tok_count :].reshape(-1)
     kv_all = lax.all_gather(kv_rows, "seq", axis=0, tiled=True)
-    states = fold_plain(states, (kv_all, seg_all, pos_all))
+    attended_heads = flash_attend(query_heads, seg_ids, positions, kv_all, seg_all, pos_all)
     block_count = tok_count // PAGE
     total_blocks = block_count * seq_count
     inverse = jnp.zeros((total_blocks,), jnp.int32).at[table_all].set(
@@ -158,8 +230,6 @@
     placed = jnp.take(kv_all.reshape(total_blocks, PAGE, 2 * width_dev), mine, axis=0)
     k_cache = placed[:, :, :width_dev]
     v_cache = placed[:, :, width_dev:]
-    finished = [finish(one_state) for one_state in states]
-    attended_heads = finished[0]
     attended = jnp.transpose(attended_heads, (1, 0, 2)).reshape(tok_count, width_dev)
     partial_out = jnp.dot(attended, w_out, preferred_element_type=jnp.float32).astype(jnp.bfloat16)
     delta = lax.psum_scatter(partial_out, "tp", scatter_dimension=1, tiled=True)

time: 303 us -> 268 us (0.88)
  matrix products: 56.1 us -> 9.81 us
  Pallas kernels: 0 us -> 45.2 us
  other arithmetic: 45.2 us -> 14.5 us
  local copies, waits for them, and re-layouts: 46.7 us -> 25.8 us
  waiting for transfers between devices: 114 us -> 133 us
    pallas_call x0 -> x1, Pallas kernels: none -> 45.2 us  [flash_attend(): pl.pallas_call(flash_kernel, grid_spec=grid_spec, out_shape=jax.ShapeDtyp...]
    reduce_sum x1 -> x0, other arithmetic: 24.9 us -> none  [attend_piece(): new_sum = jnp.sum(weights, axis=2)]
    dot_general x1 -> x0, matrix products: 22.6 us -> none  [attend_piece(): jnp.einsum('hqe,khe->hqk', query_heads, key_heads, preferred_element_type...]
    cond x1 -> x0, matrix products: 22.3 us -> none  [attend_group(): lax.cond(jnp.any(visible), attend_piece, lambda current: current, state)]
    reduce_scatter x1, waiting for transfers between devices: 28.3 us -> 48.7 us  [body(): delta = lax.psum_scatter(partial_out, 'tp', scatter_dimension=1, tiled=True)]
    all_gather x1 -> x0, local copies, waits for them, and re-layouts: 14.4 us -> none  [body(): kv_all = lax.all_gather(kv_rows, 'seq', axis=0, tiled=True)]
    unnamed x24 -> x23, local copies, waits for them, and re-layouts: 10 us -> 3.41 us
    slice x5 -> x2, local copies, waits for them, and re-layouts: 11.3 us -> 5.02 us  [the longest x1 3.28 us: rotate(): first_half = vectors[..., :half_width]]
  transfers between devices with their start and end apart: 3 -> 3, of which waited for: 3 -> 3; matrix products, arithmetic and copies ran while one was open for 11% -> 8% of each run, Pallas kernels for 0% -> 0%
where the time goes in v2:
time: 268 us; the launch traced here: 266 us
  waiting for transfers between devices  133 us (50%)
  Pallas kernels  45.2 us (17%)
  local copies, waits for them, and re-layouts  25.8 us (10%)
  blocking collectives  22.8 us (9%)
  between operations  14.6 us (5%)
  other arithmetic  14.5 us (5%)
  matrix products  9.81 us (4%)
    all_gather x1, waiting for transfers between devices, body(): lax.all_gather(hidden, 'tp', axis=1, tiled=True).astype(jnp.float32)  54.7 us
    reduce_scatter x1, waiting for transfers between devices, body(): delta = lax.psum_scatter(partial_out, 'tp', scatter_dimension=1, tiled=True)  48.7 us
    pallas_call x1, Pallas kernels, flash_attend(): pl.pallas_call(flash_kernel, grid_spec=grid_spec, out_shape=jax.ShapeDtyp...  45.2 us
    all_gather x1, waiting for transfers between devices, body(): kv_all = lax.all_gather(kv_rows, 'seq', axis=0, tiled=True)  28.7 us
    unnamed x1, blocking collectives  22.8 us
    dot_general x1, matrix products, body(): jnp.einsum('td,jde->jte', normed, w_qkv, preferred_element_type=jnp.float32)  6.74 us
  transfers between devices with their start and end apart: 3, of which 3 were waited for; matrix products, arithmetic and copies ran while one was open for 8% of the time, Pallas kernels for 0%

profile of v2, /device:TPU:5, one launch (start us, length us, event | category | flops | bytes accessed | tf_op | source)
XLA Modules:
  0.0 265.6 jit_solution(9624850766684709111)
XLA Ops:
  7.2 0.0 copy-start
  7.2 0.0 all-gather.4.cloned.1.call-start
  7.2 0.7 all-gather.4.cloned.1.call-update
  7.9 0.0 all-gather.6.cloned.1.call-start
  8.0 0.7 convert_element_type.35
  8.7 2.1 multiply_cosine_fusion
  10.7 54.7 %all-gather.4.cloned.1.call-done = bf16[640,2048]{1,0:T(8,128)(2,1)} async-done(((bf16[640,512]{1,0:T(8,128)(2,1)}), bf16[640,2048]{1,0:T(8,128)(2,1)}) %all-gather.4.cloned.1.call-update) | async-done | bytes 2621456 | tf_op jit(solution)/shard_map/all_gather | solution.py:198
  65.4 2.3 convert_reduce_fusion
  67.7 0.2 copy-done.1
  67.9 0.8 fusion.2
  68.7 6.7 %fusion.9 = f32[3,640,512]{2,1,0:T(8,128)S(1)} fusion(bf16[3,2048,512]{2,1,0:T(8,128)(2,1)} %param.7, bf16[640,2048]{1,0:T(8,128)(2,1)S(1)} %copy-done.1, f32[640]{0:T(1024)S(1)} %add_rsqrt_fusion, f32[640]{0:T(1024)S(1)} %broadcast_multiply_fusion), kind=kOutput, calls=%fused_computation.14 | convolution fusion | flops 4031774720 | bytes 12850176 | tf_op jit(solution)/shard_map/td,jde->jte/dot_general | solution.py:203
  75.5 1.7 fusion.16
  77.2 0.9 fusion.12
  78.1 1.7 reshape_squeeze.6
  79.8 2.7 %reshape_squeeze.7 = f32[640,4,128]{2,1,0:T(4,128)} reshape(f32[1,640,512]{2,1,0:T(8,128)} %get-tuple-element.5) | data formatting | bytes 2621440 | tf_op jit(solution)/shard_map/reshape;squeeze | solution.py:211
  82.5 3.3 %fusion.18 = (f32[640,4,64]{2,1,0:T(4,128)S(1)}, f32[640,4,64]{2,1,0:T(4,128)S(1)}, f32[640,4,64]{2,1,0:T(4,128)S(1)}, f32[640,4,64]{2,1,0:T(4,128)S(1)}) fusion(f32[640,4,128]{2,1,0:T(4,128)} %reshape_squeeze.7, f32[640,4,128]{2,1,0:T(4,128)S(1)} %reshape_squeeze.6), kind=kLoop, calls=%fused_computation.44 | loop fusion | bytes 5242880 | tf_op jit(solution)/shard_map/slice | solution.py:26
  85.8 0.7 subtract_convert_fusion
  86.5 0.0 copy-start.2
  86.5 0.3 copy_bitcast_fusion
  86.9 0.7 copy-done.2
  87.6 1.2 pad_maximum_fusion
  88.8 0.0 all-gather.6.cloned.1.call-update
  88.9 0.0 reduce-scatter.2.cloned.1.call-start
  88.9 0.6 copy-done.5
  89.5 0.9 broadcast_in_dim.35.qpos_ref
  90.4 0.9 broadcast_in_dim.34.qseg_ref
  91.3 0.6 dynamic-slice
  92.5 0.1 add_dynamic-update-slice_fusion
  92.7 22.8 %all-reduce = s32[10560]{0:T(1024)S(1)} all-reduce(s32[10560]{0:T(1024)S(1)} %add_dynamic-update-slice_fusion), channel_id=2, replica_groups=mesh['seq'=8,'tp'=4] {'seq'}, use_global_device_ids=true, to_apply=%add | all-reduce | flops 10560 | bytes 84480
  115.5 0.1 reshape.203
  115.6 3.3 %and_reduce_fusion = pred[8]{0:T(512)(128)(4,1)S(1)} fusion(s32[8,640]{1,0:T(8,128)S(1)} %get-tuple-element.21, s32[8,640]{1,0:T(8,128)S(1)} %get-tuple-element.22, s32[640]{0:T(1024)S(1)} %copy-done.5, s32[640]{0:T(1024)S(1)} %copy-done.6), kind=kLoop, calls=%fused_computation.2 | loop fusion | flops 13107192 | bytes 46088 | tf_op jit(solution)/shard_map/reduce_or | solution.py:121
  118.9 0.6 convert_element_type.32.need_ref
  119.5 0.6 copy.43
  120.1 0.6 copy.44
  120.8 0.8 reduce-window.9
  121.5 1.2 maximum_bitcast_fusion.q_ref
  122.7 28.7 %all-gather.6.cloned.1.call-done.k_ref.v_ref = bf16[5120,1024]{1,0:T(8,128)(2,1)} async-done(((bf16[640,1024]{1,0:T(8,128)(2,1)}), bf16[5120,1024]{1,0:T(8,128)(2,1)}) %all-gather.6.cloned.1.call-update) | async-done | bytes 10485776 | tf_op jit(solution)/shard_map/all_gather | solution.py:222
  151.4 45.2 %shard_map.85 = bf16[4,640,128]{2,1,0:T(8,128)(2,1)} custom-call(s32[8]{0:T(128)} %convert_element_type.32.need_ref, s32[8]{0:T(128)} %bitcast.39, bf16[4,640,128]{2,1,0:T(8,128)(2,1)} %maximum_bitcast_fusion.q_ref, bf16[5120,1024]{1,0:T(8,128)(2,1)} %all-gather.6.cloned.1.call-done.k_ref.v_ref, bf16[5120,1024]{1,0:T(8,128)(2,1)} %all-gather.6.cloned.1.call-done.k_ref.v_ref, ...), custom_call_target="tpu_custom_call" | custom-call | tf_op jit(solution)/shard_map/pallas_call | solution.py:142
  196.6 1.4 copy.35
  198.0 3.1 %convolution_convert_fusion = bf16[640,2048]{1,0:T(8,128)(2,1)} fusion(bf16[640,512]{0,1:T(8,128)(2,1)S(1)} %bitcast.36, bf16[512,2048]{1,0:T(8,128)(2,1)S(1)} %copy-done), kind=kOutput, calls=%fused_computation.9 | convolution fusion | flops 1343488000 | bytes 5373952 | tf_op jit(solution)/shard_map/dot_general | solution.py:234
  201.1 0.0 reduce-scatter.2.cloned.1.call-update
  201.1 0.1 reshape.185
  201.2 2.9 %scatter_custom_fusion = s32[320]{0:T(512)S(1)} fusion(s32[320]{0:T(512)S(1)} %fusion.13, s32[320]{0:T(512)S(1)} %iota.14, s32[]{:T(128)} %constant.15.clone.1), kind=kCustom, calls=%fused_computation.37 | custom fusion | bytes 1284 | tf_op jit(solution)/shard_map/scatter | solution.py:226
  204.2 0.1 compare_and_fusion
  204.3 4.6 %gather_fusion = bf16[40,16,1024]{2,1,0:T(8,128)(2,1)S(1)} fusion(bf16[320,16,1024]{2,1,0:T(8,128)(2,1)} %bitcast.34, s32[1024]{0:T(1024)S(1)} %pad_clamp_fusion), kind=kCustom, calls=%fused_computation | custom fusion | bytes 2621600 | tf_op jit(solution)/shard_map/jit(_take)/gather | solution.py:230
  208.9 0.2 broadcast_select_fusion
  209.1 1.2 fusion.17
  210.3 48.7 %reduce-scatter.2.cloned.1.call-done = bf16[640,512]{1,0:T(8,128)(2,1)} async-done(((bf16[640,2048]{1,0:T(8,128)(2,1)}), bf16[640,512]{1,0:T(8,128)(2,1)}) %reduce-scatter.2.cloned.1.call-update) | async-done | bytes 655376 | tf_op jit(solution)/shard_map/reduce_scatter | solution.py:235
  (23 shorter events, 0.1 us)
Async XLA Ops:
  7.2 190.8 %copy-start = (bf16[512,2048]{1,0:T(8,128)(2,1)S(1)}, bf16[512,2048]{1,0:T(8,128)(2,1)}, u32[]{:S(2)}) copy-start(bf16[512,2048]{1,0:T(8,128)(2,1)} %param.8) | copy-start | bytes 6291460
  7.2 58.2 %all-gather.4.cloned.1.call-start = ((), (), s32[]{:S(2)}) async-start(), calls=%async_computation.1 | async-start | bytes 3276800 | tf_op jit(solution)/shard_map/all_gather | solution.py:198
  7.9 143.5 %all-gather.6.cloned.1.call-start = ((), (), s32[]{:S(2)}) async-start(), calls=%async_computation.2 | async-start | bytes 11796480 | tf_op jit(solution)/shard_map/all_gather | solution.py:222
  65.4 2.5 copy-start.1
  82.5 3.3 %copy-start.3 = (f32[640,64]{1,0:T(8,128)S(1)}, f32[640,64]{1,0:T(8,128)}, u32[]{:S(2)}) copy-start(f32[640,64]{1,0:T(8,128)} %get-tuple-element.23) | copy-start | bytes 491524
  82.5 3.3 %copy-start.4 = (f32[640,64]{1,0:T(8,128)S(1)}, f32[640,64]{1,0:T(8,128)}, u32[]{:S(2)}) copy-start(f32[640,64]{1,0:T(8,128)} %get-tuple-element.24) | copy-start | bytes 491524
  86.5 1.1 copy-start.2
  88.8 0.7 copy-start.5
  88.8 1.6 copy-start.6
  88.8 2.4 copy-start.8
  88.8 3.7 %copy-start.7 = (s32[40]{0:T(128)S(1)}, s32[40]{0:T(128)}, u32[]{:S(2)}) copy-start(s32[40]{0:T(128)} %param.11) | copy-start | bytes 484
  88.9 170.2 %reduce-scatter.2.cloned.1.call-start = ((), (), s32[]{:S(2)}) async-start(), calls=%async_computation.3 | async-start | bytes 3276800 | tf_op jit(solution)/shard_map/reduce_scatter | solution.py:235
Sparse Core Ops, SparseCore 0:
  9.6 55.7 all-gather.3
  89.0 62.3 all-gather.5
  201.2 57.7 reduce-scatter.1

commit v3 on v2

--- a/solution.py
+++ b/solution.py
@@ -214,12 +214,16 @@
     kv_rows = jnp.concatenate([key_heads.reshape(tok_count, width_dev), values], axis=1)
     query_heads = jnp.transpose(queries, (1, 0, 2))
     seq_count = lax.axis_size("seq")
-    int_rows = jnp.concatenate([seg_ids, positions, page_table])
-    int_all = lax.all_gather(int_rows, "seq", axis=0, tiled=False)
-    seg_all = int_all[:, :tok_count].reshape(-1)
-    pos_all = int_all[:, tok_count : 2 * tok_count].reshape(-1)
-    table_all = int_all[:, 2 * tok_count :].reshape(-1)
-    kv_all = lax.all_gather(kv_rows, "seq", axis=0, tiled=True)
+    table_rows = jnp.repeat(page_table, PAGE)
+    side = jnp.stack(
+        [seg_ids, positions // 128, positions % 128, table_rows // 128, table_rows % 128], axis=1
+    )
+    side = jnp.pad(side, ((0, 0), (0, 128 - side.shape[1]))).astype(jnp.bfloat16)
+    kv_all = lax.all_gather(jnp.concatenate([kv_rows, side], axis=1), "seq", axis=0, tiled=True)
+    side_all = kv_all[:, 2 * width_dev : 2 * width_dev + 5].astype(jnp.int32)
+    seg_all = side_all[:, 0]
+    pos_all = side_all[:, 1] * 128 + side_all[:, 2]
+    table_all = (side_all[:, 3] * 128 + side_all[:, 4])[::PAGE]
     attended_heads = flash_attend(query_heads, seg_ids, positions, kv_all, seg_all, pos_all)
     block_count = tok_count // PAGE
     total_blocks = block_count * seq_count
@@ -227,9 +231,9 @@
         jnp.arange(total_blocks, dtype=jnp.int32)
     )
     mine = lax.dynamic_slice(inverse, (lax.axis_index("seq") * block_count,), (block_count,))
-    placed = jnp.take(kv_all.reshape(total_blocks, PAGE, 2 * width_dev), mine, axis=0)
+    placed = jnp.take(kv_all.reshape(total_blocks, PAGE, kv_all.shape[1]), mine, axis=0)
     k_cache = placed[:, :, :width_dev]
-    v_cache = placed[:, :, width_dev:]
+    v_cache = placed[:, :, width_dev : 2 * width_dev]
     attended = jnp.transpose(attended_heads, (1, 0, 2)).reshape(tok_count, width_dev)
     partial_out = jnp.dot(attended, w_out, preferred_element_type=jnp.float32).astype(jnp.bfloat16)
     delta = lax.psum_scatter(partial_out, "tp", scatter_dimension=1, tiled=True)

time: 268 us -> 285 us (1.063)
  waiting for transfers between devices: 133 us -> 163 us
  blocking collectives: 22.8 us -> 0 us
  other arithmetic: 14.5 us -> 23.5 us
    all_gather x1, waiting for transfers between devices: 28.7 us -> 64.4 us  [body(): lax.all_gather(jnp.concatenate([kv_rows, side], axis=1), 'seq', axis=0, t...]
    unnamed x1 -> x0, blocking collectives: 22.8 us -> none
    add x0 -> x1, other arithmetic: none -> 5.42 us  [body(): table_all = (side_all[:, 3] * 128 + side_all[:, 4])[::PAGE]]
    reduce_scatter x1, waiting for transfers between devices: 48.7 us -> 45.6 us  [body(): delta = lax.psum_scatter(partial_out, 'tp', scatter_dimension=1, tiled=True)]
  transfers between devices with their start and end apart: 3 -> 3, of which waited for: 3 -> 3; matrix products, arithmetic and copies ran while one was open for 8% -> 7% of each run, Pallas kernels for 0% -> 0%
where the time goes in v3:
time: 285 us; the launch traced here: 283 us
  waiting for transfers between devices  163 us (57%)
  Pallas kernels  45.2 us (16%)
  local copies, waits for them, and re-layouts  26.8 us (9%)
  other arithmetic  23.5 us (8%)
  between operations  14 us (5%)
  matrix products  9.89 us (3%)
    all_gather x1, waiting for transfers between devices, body(): lax.all_gather(jnp.concatenate([kv_rows, side], axis=1), 'seq', axis=0, t...  64.4 us
    all_gather x1, waiting for transfers between devices, body(): lax.all_gather(hidden, 'tp', axis=1, tiled=True).astype(jnp.float32)  52.1 us
    reduce_scatter x1, waiting for transfers between devices, body(): delta = lax.psum_scatter(partial_out, 'tp', scatter_dimension=1, tiled=True)  45.6 us
    pallas_call x1, Pallas kernels, flash_attend(): pl.pallas_call(flash_kernel, grid_spec=grid_spec, out_shape=jax.ShapeDtyp...  45.2 us
    dot_general x1, matrix products, body(): jnp.einsum('td,jde->jte', normed, w_qkv, preferred_element_type=jnp.float32)  6.74 us
    gather x1, local copies, waits for them, and re-layouts, body(): jnp.take(kv_all.reshape(total_blocks, PAGE, kv_all.shape[1]), mine, axis=0)  6.27 us
  transfers between devices with their start and end apart: 3, of which 3 were waited for; matrix products, arithmetic and copies ran while one was open for 7% of the time, Pallas kernels for 0%

profile of v3, /device:TPU:5, one launch (start us, length us, event | category | flops | bytes accessed | tf_op | source)
XLA Modules:
  0.0 282.5 jit_solution(2009941848133159069)
XLA Ops:
  7.2 0.0 copy-start
  7.2 0.0 all-gather.3.cloned.1.call-start
  7.2 0.7 all-gather.3.cloned.1.call-update
  7.9 0.0 all-gather.5.cloned.1.call-start
  8.0 0.8 fusion.29
  8.8 0.7 broadcast_in_dim.17
  9.5 0.1 reshape.288
  9.6 0.7 reshape_convert_fusion
  10.4 0.8 copy.49
  11.2 2.0 multiply_cosine_fusion
  13.2 52.1 %all-gather.3.cloned.1.call-done = bf16[640,2048]{1,0:T(8,128)(2,1)} async-done(((bf16[640,512]{1,0:T(8,128)(2,1)}), bf16[640,2048]{1,0:T(8,128)(2,1)}) %all-gather.3.cloned.1.call-update) | async-done | bytes 2621456 | tf_op jit(solution)/shard_map/all_gather | solution.py:198
  65.4 2.3 convert_reduce_fusion
  67.7 0.2 copy-done.1
  67.9 0.8 fusion.2
  68.7 6.7 %fusion.12 = f32[3,640,512]{2,1,0:T(8,128)S(1)} fusion(bf16[3,2048,512]{2,1,0:T(8,128)(2,1)} %param.7, bf16[640,2048]{1,0:T(8,128)(2,1)S(1)} %copy-done.1, f32[640]{0:T(1024)S(1)} %add_rsqrt_fusion, f32[640]{0:T(1024)S(1)} %broadcast_multiply_fusion), kind=kOutput, calls=%fused_computation.23 | convolution fusion | flops 4031774720 | bytes 12850176 | tf_op jit(solution)/shard_map/td,jde->jte/dot_general | solution.py:203
  75.5 0.9 fusion.16
  76.4 1.7 fusion.25
  78.1 1.7 reshape_squeeze.8
  79.8 2.7 reshape_squeeze.7
  82.5 3.3 %fusion.27 = (f32[640,4,64]{2,1,0:T(4,128)S(1)}, f32[640,4,64]{2,1,0:T(4,128)S(1)}, f32[640,4,64]{2,1,0:T(4,128)S(1)}, f32[640,4,64]{2,1,0:T(4,128)S(1)}) fusion(f32[640,4,128]{2,1,0:T(4,128)S(1)} %reshape_squeeze.8, f32[640,4,128]{2,1,0:T(4,128)} %reshape_squeeze.7), kind=kLoop, calls=%fused_computation.67 | loop fusion | bytes 5242880 | tf_op jit(solution)/shard_map/slice | solution.py:26
  85.8 0.0 copy-done.3
  85.8 0.7 subtract_convert_fusion
  86.5 0.0 copy-start.2
  86.5 0.3 copy_bitcast_fusion
  86.9 0.7 copy-done.2
  87.6 1.3 fusion.15
  88.9 0.0 all-gather.5.cloned.1.call-update
  88.9 0.2 reduce-scatter.2.cloned.1.call-start
  89.2 0.9 broadcast_in_dim.39.qpos_ref
  90.1 0.9 copy.52.qseg_ref
  91.0 1.2 maximum_bitcast_fusion.1.q_ref
  92.2 64.4 %all-gather.5.cloned.1.call-done.k_ref.v_ref = bf16[5120,1152]{1,0:T(8,128)(2,1)} async-done(((bf16[640,1152]{1,0:T(8,128)(2,1)}), bf16[5120,1152]{1,0:T(8,128)(2,1)}) %all-gather.5.cloned.1.call-update) | async-done | bytes 11796496 | tf_op jit(solution)/shard_map/all_gather | solution.py:222
  156.6 1.6 slice_convert_fusion
  158.2 5.4 %fusion.8 = (s32[5120]{0:T(1024)S(1)}, s32[5120]{0:T(1024)S(1)}, s32[5120]{0:T(1024)S(1)}) fusion(s32[5120,5]{1,0:T(8,128)S(1)} %slice_convert_fusion), kind=kLoop, calls=%fused_computation.15 | loop fusion | flops 20480 | bytes 163840 | tf_op jit(solution)/shard_map/add | solution.py:226
  163.6 3.3 %and_reduce_fusion = pred[8]{0:T(512)(128)(4,1)S(1)} fusion(s32[8,640]{1,0:T(8,128)S(1)} %add.93, s32[8,640]{1,0:T(8,128)S(1)} %eq.19, s32[640]{0:T(1024)S(1)} %copy-done.9, s32[640]{0:T(1024)S(1)} %copy-done.8), kind=kLoop, calls=%fused_computation.2 | loop fusion | flops 13107192 | bytes 46088 | tf_op jit(solution)/shard_map/reduce_or | solution.py:121
  167.0 0.5 convert_element_type.43.need_ref
  167.5 0.7 reduce-window.9
  168.2 45.2 %shard_map.85 = bf16[4,640,128]{2,1,0:T(8,128)(2,1)} custom-call(s32[8]{0:T(128)} %convert_element_type.43.need_ref, s32[8]{0:T(128)} %bitcast.32, bf16[4,640,128]{2,1,0:T(8,128)(2,1)} %maximum_bitcast_fusion.1.q_ref, bf16[5120,1152]{1,0:T(8,128)(2,1)} %all-gather.5.cloned.1.call-done.k_ref.v_ref, ...), custom_call_target="tpu_custom_call" | custom-call | tf_op jit(solution)/shard_map/pallas_call | solution.py:142
  213.4 1.4 copy.54
  214.8 3.2 %convolution_convert_fusion = bf16[640,2048]{1,0:T(8,128)(2,1)} fusion(bf16[640,512]{0,1:T(8,128)(2,1)S(1)} %bitcast.29, bf16[512,2048]{1,0:T(8,128)(2,1)S(1)} %copy-done), kind=kOutput, calls=%fused_computation.9 | convolution fusion | flops 1343488000 | bytes 5373952 | tf_op jit(solution)/shard_map/dot_general | solution.py:238
  218.0 0.0 reduce-scatter.2.cloned.1.call-update
  218.0 0.2 slice.62
  218.2 2.9 %scatter_custom_fusion = s32[320]{0:T(512)S(1)} fusion(s32[320]{0:T(512)S(1)} %compare_select_fusion, s32[320]{0:T(512)S(1)} %iota.14, s32[]{:T(128)} %constant.77.clone.1), kind=kCustom, calls=%fused_computation.62 | custom fusion | bytes 1284 | tf_op jit(solution)/shard_map/scatter | solution.py:230
  221.2 0.1 compare_and_fusion
  221.3 6.3 %gather_fusion = bf16[40,16,1152]{2,1,0:T(8,128)(2,1)} fusion(bf16[320,16,1152]{2,1,0:T(8,128)(2,1)} %bitcast.27, s32[1024]{0:T(1024)S(1)} %pad_clamp_fusion), kind=kCustom, calls=%fused_computation | custom fusion | bytes 2949280 | tf_op jit(solution)/shard_map/jit(_take)/gather | solution.py:234
  227.5 1.6 broadcast_select_fusion
  229.1 1.2 fusion.26
  230.4 45.6 %reduce-scatter.2.cloned.1.call-done = bf16[640,512]{1,0:T(8,128)(2,1)} async-done(((bf16[640,2048]{1,0:T(8,128)(2,1)}), bf16[640,512]{1,0:T(8,128)(2,1)}) %reduce-scatter.2.cloned.1.call-update) | async-done | bytes 655376 | tf_op jit(solution)/shard_map/reduce_scatter | solution.py:239
  (30 shorter events, 0.2 us)
Async XLA Ops:
  7.2 207.7 %copy-start = (bf16[512,2048]{1,0:T(8,128)(2,1)S(1)}, bf16[512,2048]{1,0:T(8,128)(2,1)}, u32[]{:S(2)}) copy-start(bf16[512,2048]{1,0:T(8,128)(2,1)} %param.8) | copy-start | bytes 6291460
  7.2 58.2 %all-gather.3.cloned.1.call-start = ((), (), s32[]{:S(2)}) async-start(), calls=%async_computation.1 | async-start | bytes 3276800 | tf_op jit(solution)/shard_map/all_gather | solution.py:198
  7.9 148.7 %all-gather.5.cloned.1.call-start = ((), (), s32[]{:S(2)}) async-start(), calls=%async_computation.2 | async-start | bytes 13271040 | tf_op jit(solution)/shard_map/all_gather | solution.py:222
  65.4 2.5 copy-start.1
  82.5 3.3 %copy-start.3 = (f32[640,64]{1,0:T(8,128)S(1)}, f32[640,64]{1,0:T(8,128)}, u32[]{:S(2)}) copy-start(f32[640,64]{1,0:T(8,128)} %get-tuple-element.24) | copy-start | bytes 491524
  82.5 3.3 %copy-start.4 = (f32[640,64]{1,0:T(8,128)S(1)}, f32[640,64]{1,0:T(8,128)}, u32[]{:S(2)}) copy-start(f32[640,64]{1,0:T(8,128)} %get-tuple-element.25) | copy-start | bytes 491524
  85.8 1.1 copy-start.5
  86.5 1.1 copy-start.2
  87.6 1.6 copy-start.8
  87.6 1.6 copy-start.9
  88.9 187.0 %reduce-scatter.2.cloned.1.call-start = ((), (), s32[]{:S(2)}) async-start(), calls=%async_computation.3 | async-start | bytes 3276800 | tf_op jit(solution)/shard_map/reduce_scatter | solution.py:239
  163.6 4.6 %copy-start.6 = (s32[5120]{0:T(1024)}, s32[5120]{0:T(1024)S(1)}, u32[]{:S(2)}) copy-start(s32[5120]{0:T(1024)S(1)} %get-tuple-element.4) | copy-start | bytes 61444
  163.6 4.6 %copy-start.7 = (s32[5120]{0:T(1024)}, s32[5120]{0:T(1024)S(1)}, u32[]{:S(2)}) copy-start(s32[5120]{0:T(1024)S(1)} %get-tuple-element.5) | copy-start | bytes 61444
Sparse Core Ops, SparseCore 0:
  9.6 55.7 all-gather.2
  89.1 67.4 all-gather.4
  218.1 57.8 reduce-scatter.1

commit v4 on v2

--- a/solution.py
+++ b/solution.py
@@ -82,7 +82,8 @@
 
 def flash_kernel(need_ref, kid_ref, q_ref, k_ref, v_ref, qseg_ref, qpos_ref, kseg_ref, kpos_ref,
                  o_ref, m_scr, l_scr, acc_scr):
-    j = pl.program_id(1)
+    j = pl.program_id(0)
+    head_count, _, head_width = q_ref.shape
 
     @pl.when(j == 0)
     def _():
@@ -92,22 +93,25 @@
 
     @pl.when(need_ref[j] != 0)
     def _():
-        s = lax.dot_general(
-            q_ref[...], k_ref[...], (((1,), (1,)), ((), ())), preferred_element_type=jnp.float32
-        ) * HEAD_DIM ** (-0.5)
         vis = (kseg_ref[...] == qseg_ref[...]) & (kpos_ref[...] <= qpos_ref[...])
-        s = jnp.where(vis, s, NEG_LARGE)
-        m_prev = m_scr[...]
-        m_new = jnp.maximum(m_prev, jnp.max(s, axis=1, keepdims=True))
-        alpha = jnp.exp(m_prev - m_new)
-        p = jnp.where(vis, jnp.exp(s - m_new), 0.0)
-        l_scr[...] = alpha * l_scr[...] + jnp.sum(p, axis=1, keepdims=True)
-        acc_scr[...] = alpha * acc_scr[...] + jnp.dot(
-            p.astype(jnp.bfloat16), v_ref[...], preferred_element_type=jnp.float32
-        )
-        m_scr[...] = m_new
-
-    @pl.when(j == pl.num_programs(1) - 1)
+        for h in range(head_count):
+            cols = slice(h * head_width, (h + 1) * head_width)
+            s = lax.dot_general(
+                q_ref[h], k_ref[:, cols], (((1,), (1,)), ((), ())),
+                preferred_element_type=jnp.float32,
+            ) * HEAD_DIM ** (-0.5)
+            s = jnp.where(vis, s, NEG_LARGE)
+            m_prev = m_scr[h]
+            m_new = jnp.maximum(m_prev, jnp.max(s, axis=1, keepdims=True))
+            alpha = jnp.exp(m_prev - m_new)
+            p = jnp.exp(s - m_new)
+            l_scr[h] = alpha * l_scr[h] + jnp.sum(p, axis=1, keepdims=True)
+            acc_scr[h] = alpha * acc_scr[h] + jnp.dot(
+                p.astype(jnp.bfloat16), v_ref[:, cols], preferred_element_type=jnp.float32
+            )
+            m_scr[h] = m_new
+
+    @pl.when(j == pl.num_programs(0) - 1)
     def _():
         o_ref[...] = (acc_scr[...] / l_scr[...]).astype(o_ref.dtype)
 
@@ -115,6 +119,7 @@
 def flash_attend(query_heads, seg_q, pos_q, kv_all, seg_all, pos_all):
     head_count, query_count, head_width = query_heads.shape
     key_count = kv_all.shape[0]
+    width_dev = head_count * head_width
     block_k = query_count
     block_count = key_count // block_k
     visible = (seg_all[None, :] == seg_q[:, None]) & (pos_all[None, :] <= pos_q[:, None])
@@ -122,28 +127,28 @@
     key_index = lax.cummax(jnp.where(need != 0, jnp.arange(block_count, dtype=jnp.int32), 0), axis=0)
     grid_spec = pltpu.PrefetchScalarGridSpec(
         num_scalar_prefetch=2,
-        grid=(head_count, block_count),
+        grid=(block_count,),
         in_specs=[
-            pl.BlockSpec((None, query_count, head_width), lambda h, j, nd, kd: (h, 0, 0)),
-            pl.BlockSpec((block_k, head_width), lambda h, j, nd, kd: (kd[j], h)),
-            pl.BlockSpec((block_k, head_width), lambda h, j, nd, kd: (kd[j], head_count + h)),
-            pl.BlockSpec((query_count, 1), lambda h, j, nd, kd: (0, 0)),
-            pl.BlockSpec((query_count, 1), lambda h, j, nd, kd: (0, 0)),
-            pl.BlockSpec((1, block_k), lambda h, j, nd, kd: (0, kd[j])),
-            pl.BlockSpec((1, block_k), lambda h, j, nd, kd: (0, kd[j])),
+            pl.BlockSpec((head_count, query_count, head_width), lambda j, nd, kd: (0, 0, 0)),
+            pl.BlockSpec((block_k, width_dev), lambda j, nd, kd: (kd[j], 0)),
+            pl.BlockSpec((block_k, width_dev), lambda j, nd, kd: (kd[j], 1)),
+            pl.BlockSpec((query_count, 1), lambda j, nd, kd: (0, 0)),
+            pl.BlockSpec((query_count, 1), lambda j, nd, kd: (0, 0)),
+            pl.BlockSpec((1, block_k), lambda j, nd, kd: (0, kd[j])),
+            pl.BlockSpec((1, block_k), lambda j, nd, kd: (0, kd[j])),
         ],
-        out_specs=pl.BlockSpec((None, query_count, head_width), lambda h, j, nd, kd: (h, 0, 0)),
+        out_specs=pl.BlockSpec((head_count, query_count, head_width), lambda j, nd, kd: (0, 0, 0)),
         scratch_shapes=[
-            pltpu.VMEM((query_count, 1), jnp.float32),
-            pltpu.VMEM((query_count, 1), jnp.float32),
-            pltpu.VMEM((query_count, head_width), jnp.float32),
+            pltpu.VMEM((head_count, query_count, 1), jnp.float32),
+            pltpu.VMEM((head_count, query_count, 1), jnp.float32),
+            pltpu.VMEM((head_count, query_count, head_width), jnp.float32),
         ],
     )
     return pl.pallas_call(
         flash_kernel,
         grid_spec=grid_spec,
         out_shape=jax.ShapeDtypeStruct(query_heads.shape, jnp.bfloat16),
-        compiler_params=pltpu.CompilerParams(dimension_semantics=("arbitrary", "arbitrary")),
+        compiler_params=pltpu.CompilerParams(dimension_semantics=("arbitrary",)),
         interpret=INTERPRET,
     )(
         need,

time: 268 us -> 253 us (0.944)
  Pallas kernels: 45.2 us -> 31.4 us
    pallas_call x1, Pallas kernels: 45.2 us -> 31.4 us  [flash_attend(): pl.pallas_call(flash_kernel, grid_spec=grid_spec, out_shape=jax.ShapeDtyp...]
  transfers between devices with their start and end apart: 3 -> 3, of which waited for: 3 -> 3; matrix products, arithmetic and copies ran while one was open for 8% -> 9% of each run, Pallas kernels for 0% -> 0%
where the time goes in v4:
time: 253 us; the launch traced here: 250 us
  waiting for transfers between devices  131 us (52%)
  Pallas kernels  31.4 us (12%)
  local copies, waits for them, and re-layouts  25.8 us (10%)
  blocking collectives  22.8 us (9%)
  between operations  14.6 us (6%)
  other arithmetic  14.5 us (6%)
  matrix products  9.82 us (4%)
    all_gather x1, waiting for transfers between devices, body(): lax.all_gather(hidden, 'tp', axis=1, tiled=True).astype(jnp.float32)  54.7 us
    reduce_scatter x1, waiting for transfers between devices, body(): delta = lax.psum_scatter(partial_out, 'tp', scatter_dimension=1, tiled=True)  47.3 us
    pallas_call x1, Pallas kernels, flash_attend(): pl.pallas_call(flash_kernel, grid_spec=grid_spec, out_shape=jax.ShapeDtyp...  31.4 us
    all_gather x1, waiting for transfers between devices, body(): kv_all = lax.all_gather(kv_rows, 'seq', axis=0, tiled=True)  28.7 us
    unnamed x1, blocking collectives  22.8 us
    dot_general x1, matrix products, body(): jnp.einsum('td,jde->jte', normed, w_qkv, preferred_element_type=jnp.float32)  6.74 us
  transfers between devices with their start and end apart: 3, of which 3 were waited for; matrix products, arithmetic and copies ran while one was open for 9% of the time, Pallas kernels for 0%

profile of v4, /device:TPU:5, one launch (start us, length us, event | category | flops | bytes accessed | tf_op | source)
XLA Modules:
  0.0 250.3 jit_solution(4322111782448061311)
XLA Ops:
  7.2 0.0 copy-start
  7.2 0.0 all-gather.4.cloned.1.call-start
  7.2 0.7 all-gather.4.cloned.1.call-update
  7.9 0.0 all-gather.6.cloned.1.call-start
  8.0 0.7 convert_element_type.35
  8.7 2.1 multiply_cosine_fusion
  10.7 54.7 %all-gather.4.cloned.1.call-done = bf16[640,2048]{1,0:T(8,128)(2,1)} async-done(((bf16[640,512]{1,0:T(8,128)(2,1)}), bf16[640,2048]{1,0:T(8,128)(2,1)}) %all-gather.4.cloned.1.call-update) | async-done | bytes 2621456 | tf_op jit(solution)/shard_map/all_gather | solution.py:203
  65.4 2.3 convert_reduce_fusion
  67.7 0.2 copy-done.1
  67.9 0.8 fusion.2
  68.7 6.7 %fusion.9 = f32[3,640,512]{2,1,0:T(8,128)S(1)} fusion(bf16[3,2048,512]{2,1,0:T(8,128)(2,1)} %param.7, bf16[640,2048]{1,0:T(8,128)(2,1)S(1)} %copy-done.1, f32[640]{0:T(1024)S(1)} %add_rsqrt_fusion, f32[640]{0:T(1024)S(1)} %broadcast_multiply_fusion), kind=kOutput, calls=%fused_computation.14 | convolution fusion | flops 4031774720 | bytes 12850176 | tf_op jit(solution)/shard_map/td,jde->jte/dot_general | solution.py:208
  75.5 1.7 fusion.16
  77.2 0.9 fusion.12
  78.1 1.7 reshape_squeeze.6
  79.8 2.7 %reshape_squeeze.7 = f32[640,4,128]{2,1,0:T(4,128)} reshape(f32[1,640,512]{2,1,0:T(8,128)} %get-tuple-element.5) | data formatting | bytes 2621440 | tf_op jit(solution)/shard_map/reshape;squeeze | solution.py:216
  82.5 3.3 %fusion.18 = (f32[640,4,64]{2,1,0:T(4,128)S(1)}, f32[640,4,64]{2,1,0:T(4,128)S(1)}, f32[640,4,64]{2,1,0:T(4,128)S(1)}, f32[640,4,64]{2,1,0:T(4,128)S(1)}) fusion(f32[640,4,128]{2,1,0:T(4,128)} %reshape_squeeze.7, f32[640,4,128]{2,1,0:T(4,128)S(1)} %reshape_squeeze.6), kind=kLoop, calls=%fused_computation.44 | loop fusion | bytes 5242880 | tf_op jit(solution)/shard_map/slice | solution.py:26
  85.8 0.7 subtract_convert_fusion
  86.5 0.0 copy-start.2
  86.5 0.3 copy_bitcast_fusion
  86.9 0.7 copy-done.2
  87.6 1.2 pad_maximum_fusion
  88.8 0.0 all-gather.6.cloned.1.call-update
  88.9 0.0 reduce-scatter.2.cloned.1.call-start
  88.9 0.6 copy-done.5
  89.5 0.9 broadcast_in_dim.35.qpos_ref
  90.4 0.9 broadcast_in_dim.34.qseg_ref
  91.3 0.6 dynamic-slice
  92.5 0.1 add_dynamic-update-slice_fusion
  92.7 22.8 %all-reduce = s32[10560]{0:T(1024)S(1)} all-reduce(s32[10560]{0:T(1024)S(1)} %add_dynamic-update-slice_fusion), channel_id=2, replica_groups=mesh['seq'=8,'tp'=4] {'seq'}, use_global_device_ids=true, to_apply=%add | all-reduce | flops 10560 | bytes 84480
  115.5 0.1 reshape.203
  115.6 3.3 %and_reduce_fusion = pred[8]{0:T(512)(128)(4,1)S(1)} fusion(s32[8,640]{1,0:T(8,128)S(1)} %get-tuple-element.21, s32[8,640]{1,0:T(8,128)S(1)} %get-tuple-element.22, s32[640]{0:T(1024)S(1)} %copy-done.5, s32[640]{0:T(1024)S(1)} %copy-done.6), kind=kLoop, calls=%fused_computation.2 | loop fusion | flops 13107192 | bytes 46088 | tf_op jit(solution)/shard_map/reduce_or | solution.py:126
  118.9 0.6 convert_element_type.32.need_ref
  119.5 0.6 copy.43
  120.1 0.6 copy.44
  120.8 0.8 reduce-window.9
  121.5 1.2 maximum_bitcast_fusion.q_ref
  122.7 28.7 %all-gather.6.cloned.1.call-done.k_ref.v_ref = bf16[5120,1024]{1,0:T(8,128)(2,1)} async-done(((bf16[640,1024]{1,0:T(8,128)(2,1)}), bf16[5120,1024]{1,0:T(8,128)(2,1)}) %all-gather.6.cloned.1.call-update) | async-done | bytes 10485776 | tf_op jit(solution)/shard_map/all_gather | solution.py:227
  151.4 31.4 %shard_map.85 = bf16[4,640,128]{2,1,0:T(8,128)(2,1)} custom-call(s32[8]{0:T(128)} %convert_element_type.32.need_ref, s32[8]{0:T(128)} %bitcast.39, bf16[4,640,128]{2,1,0:T(8,128)(2,1)} %maximum_bitcast_fusion.q_ref, bf16[5120,1024]{1,0:T(8,128)(2,1)} %all-gather.6.cloned.1.call-done.k_ref.v_ref, bf16[5120,1024]{1,0:T(8,128)(2,1)} %all-gather.6.cloned.1.call-done.k_ref.v_ref, ...), custom_call_target="tpu_custom_call" | custom-call | tf_op jit(solution)/shard_map/pallas_call | solution.py:147
  182.8 1.4 copy.35
  184.2 3.1 %convolution_convert_fusion = bf16[640,2048]{1,0:T(8,128)(2,1)} fusion(bf16[640,512]{0,1:T(8,128)(2,1)S(1)} %bitcast.36, bf16[512,2048]{1,0:T(8,128)(2,1)S(1)} %copy-done), kind=kOutput, calls=%fused_computation.9 | convolution fusion | flops 1343488000 | bytes 5373952 | tf_op jit(solution)/shard_map/dot_general | solution.py:239
  187.3 0.0 reduce-scatter.2.cloned.1.call-update
  187.3 0.1 reshape.185
  187.4 2.9 %scatter_custom_fusion = s32[320]{0:T(512)S(1)} fusion(s32[320]{0:T(512)S(1)} %fusion.13, s32[320]{0:T(512)S(1)} %iota.14, s32[]{:T(128)} %constant.15.clone.1), kind=kCustom, calls=%fused_computation.37 | custom fusion | bytes 1284 | tf_op jit(solution)/shard_map/scatter | solution.py:231
  190.3 0.1 compare_and_fusion
  190.4 4.6 %gather_fusion = bf16[40,16,1024]{2,1,0:T(8,128)(2,1)S(1)} fusion(bf16[320,16,1024]{2,1,0:T(8,128)(2,1)} %bitcast.34, s32[1024]{0:T(1024)S(1)} %pad_clamp_fusion), kind=kCustom, calls=%fused_computation | custom fusion | bytes 2621600 | tf_op jit(solution)/shard_map/jit(_take)/gather | solution.py:235
  195.1 0.2 broadcast_select_fusion
  195.3 1.2 fusion.17
  196.5 47.3 %reduce-scatter.2.cloned.1.call-done = bf16[640,512]{1,0:T(8,128)(2,1)} async-done(((bf16[640,2048]{1,0:T(8,128)(2,1)}), bf16[640,512]{1,0:T(8,128)(2,1)}) %reduce-scatter.2.cloned.1.call-update) | async-done | bytes 655376 | tf_op jit(solution)/shard_map/reduce_scatter | solution.py:240
  (23 shorter events, 0.1 us)
Async XLA Ops:
  7.2 177.0 %copy-start = (bf16[512,2048]{1,0:T(8,128)(2,1)S(1)}, bf16[512,2048]{1,0:T(8,128)(2,1)}, u32[]{:S(2)}) copy-start(bf16[512,2048]{1,0:T(8,128)(2,1)} %param.8) | copy-start | bytes 6291460
  7.2 58.2 %all-gather.4.cloned.1.call-start = ((), (), s32[]{:S(2)}) async-start(), calls=%async_computation.1 | async-start | bytes 3276800 | tf_op jit(solution)/shard_map/all_gather | solution.py:203
  7.9 143.5 %all-gather.6.cloned.1.call-start = ((), (), s32[]{:S(2)}) async-start(), calls=%async_computation.2 | async-start | bytes 11796480 | tf_op jit(solution)/shard_map/all_gather | solution.py:227
  65.4 2.5 %copy-start.1 = (bf16[640,2048]{1,0:T(8,128)(2,1)S(1)}, bf16[640,2048]{1,0:T(8,128)(2,1)}, u32[]{:S(2)}) copy-start(bf16[640,2048]{1,0:T(8,128)(2,1)} %all-gather.4.cloned.1.call-done) | copy-start | bytes 7864324
  82.5 3.3 %copy-start.3 = (f32[640,64]{1,0:T(8,128)S(1)}, f32[640,64]{1,0:T(8,128)}, u32[]{:S(2)}) copy-start(f32[640,64]{1,0:T(8,128)} %get-tuple-element.23) | copy-start | bytes 491524
  82.5 3.3 %copy-start.4 = (f32[640,64]{1,0:T(8,128)S(1)}, f32[640,64]{1,0:T(8,128)}, u32[]{:S(2)}) copy-start(f32[640,64]{1,0:T(8,128)} %get-tuple-element.24) | copy-start | bytes 491524
  86.5 1.1 copy-start.2
  88.8 0.7 copy-start.5
  88.8 1.6 copy-start.6
  88.8 2.4 copy-start.8
  88.8 3.7 %copy-start.7 = (s32[40]{0:T(128)S(1)}, s32[40]{0:T(128)}, u32[]{:S(2)}) copy-start(s32[40]{0:T(128)} %param.11) | copy-start | bytes 484
  88.9 154.9 %reduce-scatter.2.cloned.1.call-start = ((), (), s32[]{:S(2)}) async-start(), calls=%async_computation.3 | async-start | bytes 3276800 | tf_op jit(solution)/shard_map/reduce_scatter | solution.py:240
Sparse Core Ops, SparseCore 0:
  9.6 55.7 all-gather.3
  89.0 62.3 all-gather.5
  187.4 56.3 reduce-scatter.1

commit v5 on v4

--- a/solution.py
+++ b/solution.py
@@ -237,7 +237,11 @@
     v_cache = placed[:, :, width_dev:]
     attended = jnp.transpose(attended_heads, (1, 0, 2)).reshape(tok_count, width_dev)
     partial_out = jnp.dot(attended, w_out, preferred_element_type=jnp.float32).astype(jnp.bfloat16)
-    delta = lax.psum_scatter(partial_out, "tp", scatter_dimension=1, tiled=True)
+    tp_count = lax.axis_size("tp")
+    pieces = lax.all_to_all(
+        partial_out.reshape(tok_count, tp_count, -1), "tp", split_axis=1, concat_axis=1, tiled=True
+    )
+    delta = jnp.sum(pieces.astype(jnp.float32), axis=1).astype(jnp.bfloat16)
     return (delta, k_cache, v_cache)
 
 

time: 253 us -> 259 us (1.024)
  starting transfers between devices: 0.12 us -> 4.64 us
  other arithmetic: 14.5 us -> 17.6 us
    reduce_scatter x1 -> x0, waiting for transfers between devices: 47.3 us -> none  [body(): delta = lax.psum_scatter(partial_out, 'tp', scatter_dimension=1, tiled=True)]
    all_to_all x0 -> x1, waiting for transfers between devices: none -> 46.9 us  [body(): lax.all_to_all(partial_out.reshape(tok_count, tp_count, -1), 'tp', split_...]
    all_to_all x0 -> x1, starting transfers between devices: none -> 4.56 us  [body(): lax.all_to_all(partial_out.reshape(tok_count, tp_count, -1), 'tp', split_...]
    reduce_sum x0 -> x1, other arithmetic: none -> 3.16 us  [body(): delta = jnp.sum(pieces.astype(jnp.float32), axis=1).astype(jnp.bfloat16)]
  transfers between devices with their start and end apart: 3 -> 3, of which waited for: 3 -> 3; matrix products, arithmetic and copies ran while one was open for 9% -> 8% of each run, Pallas kernels for 0% -> 0%
where the time goes in v5:
time: 259 us; the launch traced here: 258 us
  waiting for transfers between devices  131 us (51%)
  Pallas kernels  31.4 us (12%)
  local copies, waits for them, and re-layouts  27.5 us (11%)
  blocking collectives  22.8 us (9%)
  other arithmetic  17.6 us (7%)
  between operations  14.9 us (6%)
  matrix products  8.29 us (3%)
  starting transfers between devices  4.64 us (2%)
    all_gather x1, waiting for transfers between devices, body(): lax.all_gather(hidden, 'tp', axis=1, tiled=True).astype(jnp.float32)  54.7 us
    all_to_all x1, waiting for transfers between devices, body(): lax.all_to_all(partial_out.reshape(tok_count, tp_count, -1), 'tp', split_...  46.9 us
    pallas_call x1, Pallas kernels, flash_attend(): pl.pallas_call(flash_kernel, grid_spec=grid_spec, out_shape=jax.ShapeDtyp...  31.4 us
    all_gather x1, waiting for transfers between devices, body(): kv_all = lax.all_gather(kv_rows, 'seq', axis=0, tiled=True)  28.7 us
    unnamed x1, blocking collectives  22.8 us
    dot_general x1, matrix products, body(): jnp.einsum('td,jde->jte', normed, w_qkv, preferred_element_type=jnp.float32)  6.74 us
  transfers between devices with their start and end apart: 3, of which 3 were waited for; matrix products, arithmetic and copies ran while one was open for 8% of the time, Pallas kernels for 0%

profile of v5, /device:TPU:5, one launch (start us, length us, event | category | flops | bytes accessed | tf_op | source)
XLA Modules:
  0.0 258.1 jit_solution(13338214458887988628)
XLA Ops:
  7.2 0.0 copy-start
  7.2 0.0 all-gather.4.cloned.1.call-start
  7.2 0.7 all-gather.4.cloned.1.call-update
  7.9 0.0 all-gather.6.cloned.1.call-start
  8.0 0.7 convert_element_type.37
  8.7 2.1 multiply_cosine_fusion
  10.7 54.7 %all-gather.4.cloned.1.call-done = bf16[640,2048]{1,0:T(8,128)(2,1)} async-done(((bf16[640,512]{1,0:T(8,128)(2,1)}), bf16[640,2048]{1,0:T(8,128)(2,1)}) %all-gather.4.cloned.1.call-update) | async-done | bytes 2621456 | tf_op jit(solution)/shard_map/all_gather | solution.py:203
  65.4 2.3 convert_reduce_fusion
  67.7 0.2 copy-done.1
  67.9 0.8 fusion.2
  68.7 6.7 %fusion.9 = f32[3,640,512]{2,1,0:T(8,128)S(1)} fusion(bf16[3,2048,512]{2,1,0:T(8,128)(2,1)} %param.7, bf16[640,2048]{1,0:T(8,128)(2,1)S(1)} %copy-done.1, f32[640]{0:T(1024)S(1)} %add_rsqrt_fusion, f32[640]{0:T(1024)S(1)} %broadcast_multiply_fusion), kind=kOutput, calls=%fused_computation.15 | convolution fusion | flops 4031774720 | bytes 12850176 | tf_op jit(solution)/shard_map/td,jde->jte/dot_general | solution.py:208
  75.5 0.9 fusion.12
  76.4 1.7 fusion.16
  78.1 1.7 reshape_squeeze.7
  79.8 2.7 %reshape_squeeze.6 = f32[640,4,128]{2,1,0:T(4,128)} reshape(f32[1,640,512]{2,1,0:T(8,128)} %get-tuple-element.6) | data formatting | bytes 2621440 | tf_op jit(solution)/shard_map/reshape;squeeze | solution.py:213
  82.5 3.3 %fusion.18 = (f32[640,4,64]{2,1,0:T(4,128)S(1)}, f32[640,4,64]{2,1,0:T(4,128)S(1)}, f32[640,4,64]{2,1,0:T(4,128)S(1)}, f32[640,4,64]{2,1,0:T(4,128)S(1)}) fusion(f32[640,4,128]{2,1,0:T(4,128)S(1)} %reshape_squeeze.7, f32[640,4,128]{2,1,0:T(4,128)} %reshape_squeeze.6), kind=kLoop, calls=%fused_computation.45 | loop fusion | bytes 5242880 | tf_op jit(solution)/shard_map/slice | solution.py:26
  85.8 0.7 subtract_convert_fusion
  86.5 0.3 copy_bitcast_fusion.1
  86.9 0.7 copy-done.2
  87.6 1.2 pad_maximum_fusion
  88.9 0.0 all-gather.6.cloned.1.call-update
  88.9 0.6 copy-done.5
  89.5 0.9 broadcast_in_dim.35.qpos_ref
  90.4 0.9 broadcast_in_dim.34.qseg_ref
  91.3 0.6 dynamic-slice
  92.5 0.1 add_dynamic-update-slice_fusion
  92.7 22.8 %all-reduce = s32[10560]{0:T(1024)S(1)} all-reduce(s32[10560]{0:T(1024)S(1)} %add_dynamic-update-slice_fusion), channel_id=2, replica_groups=mesh['seq'=8,'tp'=4] {'seq'}, use_global_device_ids=true, to_apply=%add | all-reduce | flops 10560 | bytes 84480
  115.5 0.1 reshape.207
  115.6 0.6 copy.57
  116.2 3.3 %and_reduce_fusion = pred[8]{0:T(512)(128)(4,1)S(1)} fusion(s32[8,640]{1,0:T(8,128)S(1)} %get-tuple-element.21, s32[8,640]{1,0:T(8,128)S(1)} %get-tuple-element.22, s32[640]{0:T(1024)S(1)} %copy-done.5, s32[640]{0:T(1024)S(1)} %copy-done.6), kind=kLoop, calls=%fused_computation.2 | loop fusion | flops 13107192 | bytes 46088 | tf_op jit(solution)/shard_map/reduce_or | solution.py:126
  119.5 0.6 convert_element_type.34.need_ref
  120.1 0.6 copy.56
  120.7 0.8 reduce-window.9
  121.5 1.2 maximum_bitcast_fusion.q_ref
  122.7 28.7 %all-gather.6.cloned.1.call-done.k_ref.v_ref = bf16[5120,1024]{1,0:T(8,128)(2,1)} async-done(((bf16[640,1024]{1,0:T(8,128)(2,1)}), bf16[5120,1024]{1,0:T(8,128)(2,1)}) %all-gather.6.cloned.1.call-update) | async-done | bytes 10485776 | tf_op jit(solution)/shard_map/all_gather | solution.py:227
  151.4 31.4 %shard_map.85 = bf16[4,640,128]{2,1,0:T(8,128)(2,1)} custom-call(s32[8]{0:T(128)} %convert_element_type.34.need_ref, s32[8]{0:T(128)} %bitcast.46, bf16[4,640,128]{2,1,0:T(8,128)(2,1)} %maximum_bitcast_fusion.q_ref, bf16[5120,1024]{1,0:T(8,128)(2,1)} %all-gather.6.cloned.1.call-done.k_ref.v_ref, bf16[5120,1024]{1,0:T(8,128)(2,1)} %all-gather.6.cloned.1.call-done.k_ref.v_ref, ...), custom_call_target="tpu_custom_call" | custom-call | tf_op jit(solution)/shard_map/pallas_call | solution.py:147
  182.8 1.4 copy.46
  184.2 1.6 convolution_convert_fusion
  185.8 1.7 copy.68
  187.5 4.6 %all-to-all-start = ((bf16[640,4,512]{2,0,1:T(8,128)(2,1)}), bf16[640,4,512]{2,0,1:T(8,128)(2,1)}, u32[]{:S(2)}, u32[]{:S(2)}) async-start(bf16[640,4,512]{2,0,1:T(8,128)(2,1)} %bitcast.40), calls=%async_computation | async-start | bytes 5242880 | tf_op jit(solution)/shard_map/all_to_all | solution.py:241
  192.0 0.1 reshape.189
  192.2 2.9 %scatter_custom_fusion = s32[320]{0:T(512)S(1)} fusion(s32[320]{0:T(512)S(1)} %fusion.13, s32[320]{0:T(512)S(1)} %iota.14, s32[]{:T(128)} %constant.14.clone.1), kind=kCustom, calls=%fused_computation.38 | custom fusion | bytes 1284 | tf_op jit(solution)/shard_map/scatter | solution.py:231
  195.1 0.1 compare_and_fusion
  195.2 4.6 %gather_fusion = bf16[40,16,1024]{2,1,0:T(8,128)(2,1)S(1)} fusion(bf16[320,16,1024]{2,1,0:T(8,128)(2,1)} %bitcast.39, s32[1024]{0:T(1024)S(1)} %pad_clamp_fusion), kind=kCustom, calls=%fused_computation | custom fusion | bytes 2621600 | tf_op jit(solution)/shard_map/jit(_take)/gather | solution.py:235
  199.8 0.2 broadcast_select_fusion
  200.0 1.2 fusion.17
  201.2 46.9 %all-to-all-done = bf16[640,4,512]{2,0,1:T(8,128)(2,1)} async-done(((bf16[640,4,512]{2,0,1:T(8,128)(2,1)}), bf16[640,4,512]{2,0,1:T(8,128)(2,1)}, u32[]{:S(2)}, u32[]{:S(2)}) %all-to-all-start) | async-done | bytes 2621472 | tf_op jit(solution)/shard_map/all_to_all | solution.py:241
  248.1 3.2 %reduce_sum.32 = bf16[640,512]{1,0:T(8,128)(2,1)} reduce(bf16[640,4,512]{2,0,1:T(8,128)(2,1)} %all-to-all-done, bf16[]{:T(256)} %constant.44.clone.1), dimensions={1}, to_apply=%region_4.5 | reduce | flops 983040 | bytes 3276802 | tf_op jit(solution)/shard_map/reduce_sum | solution.py:244
  (24 shorter events, 0.1 us)
Async XLA Ops:
  7.2 177.1 %copy-start = (bf16[512,2048]{1,0:T(8,128)(2,1)S(1)}, bf16[512,2048]{1,0:T(8,128)(2,1)}, u32[]{:S(2)}) copy-start(bf16[512,2048]{1,0:T(8,128)(2,1)} %param.8) | copy-start | bytes 6291460
  7.2 58.2 %all-gather.4.cloned.1.call-start = ((), (), s32[]{:S(2)}) async-start(), calls=%async_computation.1 | async-start | bytes 3276800 | tf_op jit(solution)/shard_map/all_gather | solution.py:203
  7.9 143.5 %all-gather.6.cloned.1.call-start = ((), (), s32[]{:S(2)}) async-start(), calls=%async_computation.2 | async-start | bytes 11796480 | tf_op jit(solution)/shard_map/all_gather | solution.py:227
  65.4 2.5 copy-start.1
  82.5 3.3 %copy-start.3 = (f32[640,64]{1,0:T(8,128)S(1)}, f32[640,64]{1,0:T(8,128)}, u32[]{:S(2)}) copy-start(f32[640,64]{1,0:T(8,128)} %get-tuple-element.23) | copy-start | bytes 491524
  82.5 3.3 %copy-start.4 = (f32[640,64]{1,0:T(8,128)S(1)}, f32[640,64]{1,0:T(8,128)}, u32[]{:S(2)}) copy-start(f32[640,64]{1,0:T(8,128)} %get-tuple-element.24) | copy-start | bytes 491524
  86.5 1.1 copy-start.2
  88.8 0.7 copy-start.5
  88.8 1.6 copy-start.6
  88.8 2.4 copy-start.8
  88.9 3.7 %copy-start.7 = (s32[40]{0:T(128)S(1)}, s32[40]{0:T(128)}, u32[]{:S(2)}) copy-start(s32[40]{0:T(128)} %param.11) | copy-start | bytes 484
  187.5 60.6 %all-to-all-start = ((bf16[640,4,512]{2,0,1:T(8,128)(2,1)}), bf16[640,4,512]{2,0,1:T(8,128)(2,1)}, u32[]{:S(2)}, u32[]{:S(2)}) async-start(bf16[640,4,512]{2,0,1:T(8,128)(2,1)} %bitcast.40), calls=%async_computation | async-start | bytes 5242880 | tf_op jit(solution)/shard_map/all_to_all | solution.py:241
Sparse Core Ops, SparseCore 0:
  9.6 55.7 all-gather.3
  89.0 62.3 all-gather.5

commit v6 on v4

--- a/solution.py
+++ b/solution.py
@@ -122,8 +122,13 @@
     width_dev = head_count * head_width
     block_k = query_count
     block_count = key_count // block_k
-    visible = (seg_all[None, :] == seg_q[:, None]) & (pos_all[None, :] <= pos_q[:, None])
-    need = jnp.any(visible.reshape(query_count, block_count, block_k), axis=(0, 2)).astype(jnp.int32)
+    seg_blocks = seg_all.reshape(block_count, block_k)
+    pos_low = jnp.min(pos_all.reshape(block_count, block_k), axis=1)
+    need = (
+        (jnp.min(seg_blocks, axis=1) <= jnp.max(seg_q))
+        & (jnp.max(seg_blocks, axis=1) >= jnp.min(seg_q))
+        & (pos_low <= jnp.max(pos_q))
+    ).astype(jnp.int32)
     key_index = lax.cummax(jnp.where(need != 0, jnp.arange(block_count, dtype=jnp.int32), 0), axis=0)
     grid_spec = pltpu.PrefetchScalarGridSpec(
         num_scalar_prefetch=2,

time: 253 us -> 257 us (1.016)
  Pallas kernels: 31.4 us -> 35.8 us
    pallas_call x1, Pallas kernels: 31.4 us -> 35.8 us  [flash_attend(): pl.pallas_call(flash_kernel, grid_spec=grid_spec, out_shape=jax.ShapeDtyp...]
    reduce_or x1 -> x0, other arithmetic: 3.31 us -> none  [flash_attend(): jnp.any(visible.reshape(query_count, block_count, block_k), axis=(0, 2))]
  transfers between devices with their start and end apart: 3 -> 3, of which waited for: 3 -> 3; matrix products, arithmetic and copies ran while one was open for 9% -> 8% of each run, Pallas kernels for 0% -> 0%
where the time goes in v6:
time: 257 us; the launch traced here: 255 us
  waiting for transfers between devices  132 us (51%)
  Pallas kernels  35.8 us (14%)
  local copies, waits for them, and re-layouts  25.7 us (10%)
  blocking collectives  22.8 us (9%)
  between operations  14.6 us (6%)
  other arithmetic  13.8 us (5%)
  matrix products  9.81 us (4%)
    all_gather x1, waiting for transfers between devices, body(): lax.all_gather(hidden, 'tp', axis=1, tiled=True).astype(jnp.float32)  53.9 us
    reduce_scatter x1, waiting for transfers between devices, body(): delta = lax.psum_scatter(partial_out, 'tp', scatter_dimension=1, tiled=True)  47.3 us
    pallas_call x1, Pallas kernels, flash_attend(): pl.pallas_call(flash_kernel, grid_spec=grid_spec, out_shape=jax.ShapeDtyp...  35.8 us
    all_gather x1, waiting for transfers between devices, body(): kv_all = lax.all_gather(kv_rows, 'seq', axis=0, tiled=True)  30.1 us
    unnamed x1, blocking collectives  22.8 us
    dot_general x1, matrix products, body(): jnp.einsum('td,jde->jte', normed, w_qkv, preferred_element_type=jnp.float32)  6.74 us
  transfers between devices with their start and end apart: 3, of which 3 were waited for; matrix products, arithmetic and copies ran while one was open for 8% of the time, Pallas kernels for 0%

profile of v6, /device:TPU:5, one launch (start us, length us, event | category | flops | bytes accessed | tf_op | source)
XLA Modules:
  0.0 254.8 jit_solution(13572772398666665879)
XLA Ops:
  7.2 0.0 copy-start
  7.2 0.0 all-gather.4.cloned.1.call-start
  7.2 0.7 all-gather.4.cloned.1.call-update
  7.9 0.0 all-gather.6.cloned.1.call-start
  8.0 1.5 fusion.16
  9.5 2.0 multiply_cosine_fusion
  11.5 53.9 %all-gather.4.cloned.1.call-done = bf16[640,2048]{1,0:T(8,128)(2,1)} async-done(((bf16[640,512]{1,0:T(8,128)(2,1)}), bf16[640,2048]{1,0:T(8,128)(2,1)}) %all-gather.4.cloned.1.call-update) | async-done | bytes 2621456 | tf_op jit(solution)/shard_map/all_gather | solution.py:208
  65.4 2.3 convert_reduce_fusion
  67.7 0.2 copy-done.1
  67.9 0.8 fusion.2
  68.7 6.7 %fusion.9 = f32[3,640,512]{2,1,0:T(8,128)S(1)} fusion(bf16[3,2048,512]{2,1,0:T(8,128)(2,1)} %param.7, bf16[640,2048]{1,0:T(8,128)(2,1)S(1)} %copy-done.1, f32[640]{0:T(1024)S(1)} %add_rsqrt_fusion, f32[640]{0:T(1024)S(1)} %broadcast_multiply_fusion), kind=kOutput, calls=%fused_computation.13 | convolution fusion | flops 4031774720 | bytes 12850176 | tf_op jit(solution)/shard_map/td,jde->jte/dot_general | solution.py:213
  75.5 1.7 fusion.17
  77.2 0.9 fusion.12
  78.1 1.7 reshape_squeeze.6
  79.8 2.7 %reshape_squeeze.7 = f32[640,4,128]{2,1,0:T(4,128)} reshape(f32[1,640,512]{2,1,0:T(8,128)} %get-tuple-element.12) | data formatting | bytes 2621440 | tf_op jit(solution)/shard_map/reshape;squeeze | solution.py:221
  82.5 3.3 %fusion.19 = (f32[640,4,64]{2,1,0:T(4,128)S(1)}, f32[640,4,64]{2,1,0:T(4,128)S(1)}, f32[640,4,64]{2,1,0:T(4,128)S(1)}, f32[640,4,64]{2,1,0:T(4,128)S(1)}) fusion(f32[640,4,128]{2,1,0:T(4,128)} %reshape_squeeze.7, f32[640,4,128]{2,1,0:T(4,128)S(1)} %reshape_squeeze.6), kind=kLoop, calls=%fused_computation.48 | loop fusion | bytes 5242880 | tf_op jit(solution)/shard_map/slice | solution.py:26
  85.8 0.7 subtract_convert_fusion
  86.5 0.0 copy-start.2
  86.5 0.3 copy_bitcast_fusion
  86.9 0.7 copy-done.2
  87.6 1.2 pad_maximum_fusion
  88.8 0.0 all-gather.6.cloned.1.call-update
  88.9 0.0 reduce-scatter.2.cloned.1.call-start
  88.9 0.6 copy-done.5
  89.5 0.9 reshape.225.qseg_ref
  90.4 0.9 reshape.226.qpos_ref
  91.3 0.6 dynamic-slice
  92.5 0.1 add_dynamic-update-slice_fusion
  92.7 22.8 %all-reduce = s32[10560]{0:T(1024)S(1)} all-reduce(s32[10560]{0:T(1024)S(1)} %add_dynamic-update-slice_fusion), channel_id=2, replica_groups=mesh['seq'=8,'tp'=4] {'seq'}, use_global_device_ids=true, to_apply=%add | all-reduce | flops 10560 | bytes 84480
  115.5 0.1 reshape.217
  115.6 0.2 slice_bitcast_fusion
  115.7 0.6 copy.33
  116.4 0.6 copy.34
  117.0 2.4 bitcast_select_fusion
  119.4 0.7 reduce-window.9
  120.1 1.2 maximum_bitcast_fusion.q_ref
  121.3 30.1 %all-gather.6.cloned.1.call-done.k_ref.v_ref = bf16[5120,1024]{1,0:T(8,128)(2,1)} async-done(((bf16[640,1024]{1,0:T(8,128)(2,1)}), bf16[5120,1024]{1,0:T(8,128)(2,1)}) %all-gather.6.cloned.1.call-update) | async-done | bytes 10485776 | tf_op jit(solution)/shard_map/all_gather | solution.py:232
  151.4 35.8 %shard_map.85 = bf16[4,640,128]{2,1,0:T(8,128)(2,1)} custom-call(s32[8]{0:T(128)} %get-tuple-element.11.need_ref, s32[8]{0:T(128)} %bitcast.39, bf16[4,640,128]{2,1,0:T(8,128)(2,1)} %maximum_bitcast_fusion.q_ref, bf16[5120,1024]{1,0:T(8,128)(2,1)} %all-gather.6.cloned.1.call-done.k_ref.v_ref, bf16[5120,1024]{1,0:T(8,128)(2,1)} %all-gather.6.cloned.1.call-done.k_ref.v_ref, ...), custom_call_target="tpu_custom_call" | custom-call | tf_op jit(solution)/shard_map/pallas_call | solution.py:152
  187.3 1.4 copy.25
  188.6 3.1 %convolution_convert_fusion = bf16[640,2048]{1,0:T(8,128)(2,1)} fusion(bf16[640,512]{0,1:T(8,128)(2,1)S(1)} %bitcast.36, bf16[512,2048]{1,0:T(8,128)(2,1)S(1)} %copy-done), kind=kOutput, calls=%fused_computation.8 | convolution fusion | flops 1343488000 | bytes 5373952 | tf_op jit(solution)/shard_map/dot_general | solution.py:244
  191.7 0.0 reduce-scatter.2.cloned.1.call-update
  191.8 0.1 reshape.196
  191.9 2.9 %scatter_custom_fusion = s32[320]{0:T(512)S(1)} fusion(s32[320]{0:T(512)S(1)} %fusion.13, s32[320]{0:T(512)S(1)} %iota.14, s32[]{:T(128)} %constant.16.clone.1), kind=kCustom, calls=%fused_computation.42 | custom fusion | bytes 1284 | tf_op jit(solution)/shard_map/scatter | solution.py:236
  194.8 0.1 compare_and_fusion
  194.9 4.6 %gather_fusion = bf16[40,16,1024]{2,1,0:T(8,128)(2,1)S(1)} fusion(bf16[320,16,1024]{2,1,0:T(8,128)(2,1)} %bitcast.34, s32[1024]{0:T(1024)S(1)} %pad_clamp_fusion), kind=kCustom, calls=%fused_computation | custom fusion | bytes 2621600 | tf_op jit(solution)/shard_map/jit(_take)/gather | solution.py:240
  199.5 0.2 broadcast_select_fusion
  199.7 1.2 fusion.18
  200.9 47.3 %reduce-scatter.2.cloned.1.call-done = bf16[640,512]{1,0:T(8,128)(2,1)} async-done(((bf16[640,2048]{1,0:T(8,128)(2,1)}), bf16[640,512]{1,0:T(8,128)(2,1)}) %reduce-scatter.2.cloned.1.call-update) | async-done | bytes 655376 | tf_op jit(solution)/shard_map/reduce_scatter | solution.py:245
  (21 shorter events, 0.1 us)
Async XLA Ops:
  7.2 181.5 %copy-start = (bf16[512,2048]{1,0:T(8,128)(2,1)S(1)}, bf16[512,2048]{1,0:T(8,128)(2,1)}, u32[]{:S(2)}) copy-start(bf16[512,2048]{1,0:T(8,128)(2,1)} %param.8) | copy-start | bytes 6291460
  7.2 58.2 %all-gather.4.cloned.1.call-start = ((), (), s32[]{:S(2)}) async-start(), calls=%async_computation.1 | async-start | bytes 3276800 | tf_op jit(solution)/shard_map/all_gather | solution.py:208
  7.9 143.5 %all-gather.6.cloned.1.call-start = ((), (), s32[]{:S(2)}) async-start(), calls=%async_computation.2 | async-start | bytes 11796480 | tf_op jit(solution)/shard_map/all_gather | solution.py:232
  65.4 2.5 copy-start.1
  82.5 3.3 %copy-start.3 = (f32[640,64]{1,0:T(8,128)S(1)}, f32[640,64]{1,0:T(8,128)}, u32[]{:S(2)}) copy-start(f32[640,64]{1,0:T(8,128)} %get-tuple-element.31) | copy-start | bytes 491524
  82.5 3.3 %copy-start.4 = (f32[640,64]{1,0:T(8,128)S(1)}, f32[640,64]{1,0:T(8,128)}, u32[]{:S(2)}) copy-start(f32[640,64]{1,0:T(8,128)} %get-tuple-element.32) | copy-start | bytes 491524
  86.5 1.1 copy-start.2
  88.8 0.7 copy-start.5
  88.8 1.6 copy-start.6
  88.8 2.4 copy-start.8
  88.8 3.7 %copy-start.7 = (s32[40]{0:T(128)S(1)}, s32[40]{0:T(128)}, u32[]{:S(2)}) copy-start(s32[40]{0:T(128)} %param.11) | copy-start | bytes 484
  88.9 159.4 %reduce-scatter.2.cloned.1.call-start = ((), (), s32[]{:S(2)}) async-start(), calls=%async_computation.3 | async-start | bytes 3276800 | tf_op jit(solution)/shard_map/reduce_scatter | solution.py:245
Sparse Core Ops, SparseCore 0:
  9.6 55.7 all-gather.3
  89.0 62.3 all-gather.5
  191.9 56.3 reduce-scatter.1
